TPU v7x, 256 devices: a whole 4x4x8 slice. The times are simulated.
256 devices in a mesh: seq: 64 (over x, z, core), head: 4 (over y).
Axes of the slice: x: 4, y: 4, z: 8, core: 2. Of those that a mesh axis runs over, the one named last changes fastest.
Arguments:
- query_rows: bfloat16 [8192, 2048], P(('seq', 'head')), may hold values from -160 to 160
- key_rows: bfloat16 [8192, 2048], P(('seq', 'head')), may hold values from -6 to 6
- value_rows: bfloat16 [8192, 2048], P(('seq', 'head')), may hold values from -6 to 6
- out_grad: bfloat16 [8192, 2048], P('seq', 'head'), may hold values from -48 to 48
- random_blocks: int32 [16, 64, 3], P('head'), may hold values from 0 to 63, as said below
Outputs:
- attended: bfloat16 [8192, 2048], P('seq', 'head')
- query_grad: bfloat16 [8192, 2048], P('seq', 'head')
- key_grad: bfloat16 [8192, 2048], P('seq', 'head')
- value_grad: bfloat16 [8192, 2048], P('seq', 'head')
Inputs may be any that keep to these rules, and one draw needn't show every extreme that they name: `random_blocks`: take the 4 heads of one index of head and the 1 query block of one index of seq: among their 12 entries, at most 2 equal k for any k (so at most 2 are held by any one index of seq), and for every such group of entries some k occurs exactly twice.
All inputs are finite; a program needn't handle non-finite values.
Results may differ from a plain program's by a relative error of at most 0.029.
Values may be sent and summed in bfloat16 or wider, within the bound.
A program may use at most 128 MiB of HBM per device.

v0:
```python
import math

import jax
import jax.numpy as jnp
from jax import lax
from jax.sharding import PartitionSpec as P

HD = 128
BLK = 128


def padded(x, sides, width):
    for axis, dim in sides:
        count, length = (lax.axis_size(axis), x.shape[dim])
        up = [(i, (i + 1) % count) for i in range(count)]
        down = [(j, i) for i, j in up]
        last = lax.slice_in_dim(x, length - width, length, axis=dim)
        initial = lax.slice_in_dim(x, 0, width, axis=dim)
        before = lax.ppermute(last, axis, up)
        after = lax.ppermute(initial, axis, down)
        x = jnp.concatenate([before, x, after], axis=dim)
    return x


def broadcast(block, axis, source):
    block = jnp.where(lax.axis_index(axis) == source, block, jnp.zeros_like(block))
    return lax.psum(block, axis)


def widen(blocked):
    return padded(blocked, (("seq", 0),), 1)


def spread(single, source):
    return broadcast(single, "seq", source)


def trade(buffer):
    return lax.all_to_all(buffer, "seq", split_axis=0, concat_axis=0, tiled=True)


def as_tiles(matrix, nblock, nheads):
    return matrix.reshape(nblock, BLK, nheads, HD).transpose(0, 2, 1, 3)


def as_matrix(tileset):
    nblock, nheads = (tileset.shape[0], tileset.shape[1])
    return tileset.transpose(0, 2, 1, 3).reshape(nblock * BLK, nheads * HD)


def key_set(extended, opening, closing, fetched):
    nblock = fetched.shape[0]
    nheads = fetched.shape[1]
    leading = opening[None, :, None]
    trailing = closing[None, :, None]
    window = jnp.stack([extended[:-2], extended[1:-1], extended[2:]], axis=2)
    gathered = jnp.concatenate([leading, trailing, window, fetched], axis=2)
    keys_all = gathered[:, :, :, 0].reshape(nblock, nheads, 8 * BLK, HD)
    values_all = gathered[:, :, :, 1].reshape(nblock, nheads, 8 * BLK, HD)
    return (keys_all, values_all)


def on_device(query_rows, key_rows, value_rows, out_grad, random_blocks):
    score_scale = 1.0 / math.sqrt(HD)
    query_mat, key_mat, value_mat = (
        lax.all_to_all(query_rows, "head", split_axis=1, concat_axis=0, tiled=True),
        lax.all_to_all(key_rows, "head", split_axis=1, concat_axis=0, tiled=True),
        lax.all_to_all(value_rows, "head", split_axis=1, concat_axis=0, tiled=True),
    )
    nblock = query_mat.shape[0] // BLK
    nheads = query_mat.shape[1] // HD
    seq_count = lax.axis_size("seq")
    capacity = max(2, 3 * nblock * nheads // seq_count + 1)
    item_count = 3 * nblock * nheads
    own_index = lax.axis_index("seq")
    query_tiles = as_tiles(query_mat, nblock, nheads)
    grad_tiles = as_tiles(out_grad, nblock, nheads)
    kv_tiles = jnp.stack(
        [as_tiles(key_mat, nblock, nheads), as_tiles(value_mat, nblock, nheads)], axis=2
    )
    extended = widen(kv_tiles)
    opening = spread(kv_tiles[0], 0)
    closing = spread(kv_tiles[-1], seq_count - 1)
    requests = (
        random_blocks.reshape(nheads, seq_count, nblock, 3)
        .transpose(1, 0, 2, 3)
        .reshape(seq_count, item_count)
    )
    owners = requests // nblock
    owner_hits = (owners[:, :, None] == jnp.arange(seq_count)[None, None, :]).astype(jnp.int32)
    earlier = jnp.cumsum(owner_hits, axis=1) - owner_hits
    ranks = jnp.sum(earlier * owner_hits, axis=2)
    slot_ids = jnp.arange(capacity)
    item_head = jnp.arange(item_count) // (nblock * 3)
    local_index = (requests - own_index * nblock) * nheads + item_head[None, :]
    chosen = (owners == own_index)[:, None, :] & (ranks[:, None, :] == slot_ids[None, :, None])
    send_index = jnp.sum(jnp.where(chosen, local_index[:, None, :], 0), axis=2).reshape(-1)
    send_valid = jnp.any(chosen, axis=2).reshape(-1)
    kv_flat = kv_tiles.reshape(nblock * nheads, 2, BLK, HD)
    outgoing = jnp.where(
        send_valid[:, None, None, None],
        jnp.take(kv_flat, send_index, axis=0),
        jnp.zeros((), jnp.bfloat16),
    )
    my_owners = lax.dynamic_index_in_dim(owners, own_index, 0, keepdims=False)
    my_ranks = lax.dynamic_index_in_dim(ranks, own_index, 0, keepdims=False)
    positions = my_owners * capacity + my_ranks

    def place(received):
        picked = jnp.take(received, positions, axis=0)
        return picked.reshape(nheads, nblock, 3, 2, BLK, HD).transpose(1, 0, 2, 3, 4, 5)

    fetched = place(trade(outgoing))
    keys_all, values_all = key_set(extended, opening, closing, fetched)
    scores = (
        jnp.einsum("bhqd,bhkd->bhqk", query_tiles, keys_all, preferred_element_type=jnp.float32)
        * score_scale
    )
    peaks = jnp.max(scores, axis=-1, keepdims=True)
    exponent = jnp.exp(scores - peaks)
    weights = exponent / jnp.sum(exponent, axis=-1, keepdims=True)
    rounded = weights.astype(jnp.bfloat16)
    attended = jnp.einsum(
        "bhqk,bhkd->bhqd", rounded, values_all, preferred_element_type=jnp.float32
    ).astype(jnp.bfloat16)
    refetched = place(trade(outgoing))
    back_keys, back_values = key_set(extended, opening, closing, refetched)
    row_delta = jnp.sum(grad_tiles.astype(jnp.float32) * attended.astype(jnp.float32), axis=-1)
    value_terms = jnp.einsum(
        "bhqk,bhqd->bhkd", rounded, grad_tiles, preferred_element_type=jnp.float32
    )
    prob_grad = jnp.einsum(
        "bhqd,bhkd->bhqk", grad_tiles, back_values, preferred_element_type=jnp.float32
    )
    score_grad = (weights * (prob_grad - row_delta[..., None])).astype(jnp.bfloat16)
    query_grad = (
        jnp.einsum("bhqk,bhkd->bhqd", score_grad, back_keys, preferred_element_type=jnp.float32)
        * score_scale
    ).astype(jnp.bfloat16)
    key_terms = (
        jnp.einsum("bhqk,bhqd->bhkd", score_grad, query_tiles, preferred_element_type=jnp.float32)
        * score_scale
    )
    terms = jnp.stack(
        [
            key_terms.reshape(nblock, nheads, 8, BLK, HD),
            value_terms.reshape(nblock, nheads, 8, BLK, HD),
        ],
        axis=3,
    )
    global_part = jnp.sum(terms[:, :, 0:2], axis=0).transpose(1, 0, 2, 3, 4)
    global_total = lax.psum(global_part, "seq")
    own_part = terms[:, :, 3]
    lower = terms[:, :, 2].astype(jnp.bfloat16)
    upper = terms[:, :, 4].astype(jnp.bfloat16)
    rims = widen(jnp.stack([lower[0], upper[-1]], axis=0))
    zero_tile = jnp.zeros_like(own_part)
    inner = own_part + jnp.concatenate([zero_tile, upper[:-1].astype(jnp.float32)], axis=0)
    inner = inner + jnp.concatenate([lower[1:].astype(jnp.float32), zero_tile], axis=0)
    head_add = rims[0].astype(jnp.float32) + jnp.where(own_index == 0, global_total[0], 0.0)
    tail_add = rims[-1].astype(jnp.float32) + jnp.where(
        own_index == seq_count - 1, global_total[1], 0.0
    )
    inner = inner.at[0].add(head_add).at[-1].add(tail_add)
    random_terms = (
        terms[:, :, 5:8]
        .astype(jnp.bfloat16)
        .transpose(1, 0, 2, 3, 4, 5)
        .reshape(item_count, 2, BLK, HD)
    )
    back_chosen = (my_owners[None, None, :] == jnp.arange(seq_count)[:, None, None]) & (
        my_ranks[None, None, :] == slot_ids[None, :, None]
    )
    back_index = jnp.sum(
        jnp.where(back_chosen, jnp.arange(item_count)[None, None, :], 0), axis=2
    ).reshape(-1)
    back_valid = jnp.any(back_chosen, axis=2).reshape(-1)
    returning = jnp.where(
        back_valid[:, None, None, None],
        jnp.take(random_terms, back_index, axis=0),
        jnp.zeros((), jnp.bfloat16),
    )
    returned = trade(returning)
    targets = (send_index[None, :] == jnp.arange(nblock * nheads)[:, None]) & send_valid[None, :]
    random_sum = jnp.dot(
        targets.astype(jnp.bfloat16),
        returned.reshape(seq_count * capacity, 2 * BLK * HD),
        preferred_element_type=jnp.float32,
    )
    inner = inner + random_sum.reshape(nblock, nheads, 2, BLK, HD)
    key_grad = as_matrix(inner[:, :, 0].astype(jnp.bfloat16))
    value_grad = as_matrix(inner[:, :, 1].astype(jnp.bfloat16))
    return (as_matrix(attended), as_matrix(query_grad), key_grad, value_grad)


def solution(mesh):
    in_specs = (
        P(("seq", "head"), None),
        P(("seq", "head"), None),
        P(("seq", "head"), None),
        P("seq", "head"),
        P("head", None, None),
    )
    out_specs = (P("seq", "head"), P("seq", "head"), P("seq", "head"), P("seq", "head"))
    return jax.shard_map(
        on_device, mesh=mesh, in_specs=in_specs, out_specs=out_specs, check_vma=False
    )
```

profile of v0, /device:TPU:1, one launch (start us, length us, event | category | flops | bytes accessed | tf_op | source)
XLA Modules:
  0.0 564.6 jit_solution(1573524047941959852)
XLA Ops:
  8.7 5.0 all-to-all-start
  20.0 4.2 all-to-all-start.1
  24.3 4.8 all-to-all-done.1
  29.1 3.3 all-to-all-start.3
  32.6 6.3 %gather_fusion = bf16[128,2,128,128]{3,2,1,0:T(8,128)(2,1)} fusion(bf16[4,2,128,128]{3,2,1,0:T(8,128)(2,1)S(1)} %get-tuple-element.59, s32[1024]{0:T(1024)S(1)} %pad_clamp_fusion.2), kind=kCustom, calls=%fused_computation.1 | custom fusion | bytes 16777728 | tf_op jit(solution)/shard_map/jit(_take)/gather | solution.py:102
  38.8 7.5 %select_select_fusion.1 = bf16[128,2,128,128]{3,2,1,0:T(8,128)(2,1)} fusion(bf16[128,2,128,128]{3,2,1,0:T(8,128)(2,1)} %gather_fusion, pred[128]{0:T(512)(128)(4,1)S(1)} %get-tuple-element.68, pred[128]{0:T(512)(128)(4,1)S(1)} %broadcast_in_dim.102), kind=kLoop, calls=%fused_computation.7 | loop fusion | flops 8388608 | bytes 16777472 | tf_op jit(solution)/shard_map/jit(_where)/select_n | solution.py:100
  46.4 14.5 %all-to-all-start.2 = ((bf16[128,2,128,128]{3,2,1,0:T(8,128)(2,1)}), bf16[128,2,128,128]{3,2,1,0:T(8,128)(2,1)}, u32[]{:S(2)}, u32[]{:S(2)}) async-start(bf16[128,2,128,128]{3,2,1,0:T(8,128)(2,1)} %select_select_fusion.1), calls=%async_computation.2 | async-start | bytes 16777216 | tf_op jit(solution)/shard_map/all_to_all | solution.py:39
  62.3 1.7 collective-permute-start
  64.1 210.7 %all-reduce.6.cloned.1.call-done = (bf16[1,4,1,2,128,128]{5,4,3,1,2,0:T(8,128)(2,1)}, bf16[1,4,1,2,128,128]{5,4,3,1,2,0:T(8,128)(2,1)}) async-done(((bf16[1,4,1,2,128,128]{5,4,3,1,2,0:T(8,128)(2,1)}, bf16[1,4,1,2,128,128]{5,4,3,1,2,0:T(8,128)(2,1)}), (bf16[1,4,1,2,128,128]{5,4,3,1,2,0:T(8,128)(2,1)}, bf16[1,4,1,2,128,128]{5,4,3,1,2,0:T(8,128)(2,1)})) %all-reduce.6.cloned.1.call-update) | async-done | bytes 524304 | tf_op jit(solution)/shard_map/psum | solution.py:27
  276.5 1.7 bitcast_dynamic-update-slice_fusion.3
  280.5 4.1 gather_fusion.2
  287.9 2.0 fusion.58
  289.9 4.3 fusion.44
  294.2 3.4 multiply_reduce_fusion
  297.6 2.4 fusion.3
  306.9 6.3 %gather_fusion.1 = bf16[128,2,128,128]{3,2,1,0:T(8,128)(2,1)} fusion(bf16[12,2,128,128]{3,2,1,0:T(8,128)(2,1)S(1)} %bitcast.194, s32[1024]{0:T(1024)S(1)} %pad_clamp_fusion), kind=kCustom, calls=%fused_computation.2 | custom fusion | bytes 16777728 | tf_op jit(solution)/shard_map/jit(_take)/gather | solution.py:180
  313.2 7.6 %select_select_fusion = bf16[128,2,128,128]{3,2,1,0:T(8,128)(2,1)} fusion(bf16[128,2,128,128]{3,2,1,0:T(8,128)(2,1)} %gather_fusion.1, pred[128]{0:T(512)(128)(4,1)S(1)} %get-tuple-element.67, pred[128]{0:T(512)(128)(4,1)S(1)} %broadcast_in_dim.110), kind=kLoop, calls=%fused_computation.6 | loop fusion | flops 8388608 | bytes 16777472 | tf_op jit(solution)/shard_map/jit(_where)/select_n | solution.py:178
  320.7 11.0 %all-to-all-start.4 = ((bf16[128,2,128,128]{3,2,1,0:T(8,128)(2,1)}), bf16[128,2,128,128]{3,2,1,0:T(8,128)(2,1)}, u32[]{:S(2)}, u32[]{:S(2)}) async-start(bf16[128,2,128,128]{3,2,1,0:T(8,128)(2,1)} %select_select_fusion), calls=%async_computation.4 | async-start | bytes 16777216 | tf_op jit(solution)/shard_map/all_to_all | solution.py:39
  332.0 2.3 slice_bitcast_fusion
  335.5 1.7 collective-permute-start.2
  339.2 184.7 %all-to-all-done.4 = bf16[128,2,128,128]{3,2,1,0:T(8,128)(2,1)} async-done(((bf16[128,2,128,128]{3,2,1,0:T(8,128)(2,1)}), bf16[128,2,128,128]{3,2,1,0:T(8,128)(2,1)}, u32[]{:S(2)}, u32[]{:S(2)}) %all-to-all-start.4) | async-done | bytes 8388640 | tf_op jit(solution)/shard_map/all_to_all | solution.py:39
  523.9 12.7 %copy.148 = bf16[128,2,128,128]{0,3,2,1:T(8,128)(2,1)} copy(bf16[128,2,128,128]{3,2,1,0:T(8,128)(2,1)} %all-to-all-done.4) | data formatting | bytes 16777216 | tf_op jit(solution)/shard_map/all_to_all | solution.py:39
  536.6 13.7 %all-reduce.4.cloned.1.call-done = f32[2,4,2,128,128]{4,1,3,2,0:T(4,128)} async-done(((f32[2,4,2,128,128]{4,1,3,2,0:T(4,128)}), f32[2,4,2,128,128]{4,1,3,2,0:T(4,128)}) %all-reduce.4.cloned.1.call-update) | async-done | bytes 1048592 | tf_op jit(solution)/shard_map/psum | solution.py:152
  550.3 6.0 %fusion.22 = bf16[1,4,2,128,128]{4,1,3,2,0:T(4,128)(2,1)S(1)} fusion(f32[2,4,2,128,128]{4,1,3,2,0:T(4,128)} %all-reduce.4.cloned.1.call-done, pred[]{:T(512)S(6)} %eq.94, bf16[1,4,2,128,128]{4,1,3,2,0:T(4,128)(2,1)S(1)} %collective-permute-done.3, pred[]{:T(512)S(6)} %eq.93, bf16[1,4,2,128,128]{4,1,3,2,0:T(4,128)(2,1)S(1)} %collective-permute-done.2, ...), kind=kOutput, calls=%fused_computation.52 | convolution fusion | flops 34866176 | bytes 10748546 | tf_op jit(solution)/shard_map/dot_general | solution.py:185
  (86 shorter events, 28.5 us)
Async XLA Ops:
  8.7 11.3 %all-to-all-start = ((bf16[32,4,512]{2,0,1:T(8,128)(2,1)}), bf16[32,4,512]{2,0,1:T(8,128)(2,1)S(1)}, u32[]{:S(2)}, u32[]{:S(2)}) async-start(bf16[32,4,512]{2,0,1:T(8,128)(2,1)} %bitcast.193), calls=%async_computation | async-start | bytes 262144 | tf_op jit(solution)/shard_map/all_to_all | solution.py:67
  20.0 9.1 %all-to-all-start.1 = ((bf16[32,4,512]{2,0,1:T(8,128)(2,1)}), bf16[32,4,512]{2,0,1:T(8,128)(2,1)S(1)}, u32[]{:S(2)}, u32[]{:S(2)}) async-start(bf16[32,4,512]{2,0,1:T(8,128)(2,1)} %bitcast.192), calls=%async_computation.1 | async-start | bytes 262144 | tf_op jit(solution)/shard_map/all_to_all | solution.py:68
  29.1 17.3 %all-to-all-start.3 = ((bf16[32,4,512]{2,0,1:T(8,128)(2,1)}), bf16[32,4,512]{2,0,1:T(8,128)(2,1)S(1)}, u32[]{:S(2)}, u32[]{:S(2)}) async-start(bf16[32,4,512]{2,0,1:T(8,128)(2,1)} %bitcast.191), calls=%async_computation.3 | async-start | bytes 262144 | tf_op jit(solution)/shard_map/all_to_all | solution.py:66
  46.4 15.8 %copy-start.5 = (bf16[128,512]{1,0:T(8,128)(2,1)S(1)}, bf16[128,512]{1,0:T(8,128)(2,1)}, u32[]{:S(2)}) copy-start(bf16[128,512]{1,0:T(8,128)(2,1)} %param.14) | copy-start | bytes 393220
  46.4 234.1 %all-to-all-start.2 = ((bf16[128,2,128,128]{3,2,1,0:T(8,128)(2,1)}), bf16[128,2,128,128]{3,2,1,0:T(8,128)(2,1)}, u32[]{:S(2)}, u32[]{:S(2)}) async-start(bf16[128,2,128,128]{3,2,1,0:T(8,128)(2,1)} %select_select_fusion.1), calls=%async_computation.2 | async-start | bytes 16777216 | tf_op jit(solution)/shard_map/all_to_all | solution.py:39
  60.9 214.0 %all-reduce.6.cloned.1.call-start = ((), (), s32[]{:S(2)}) async-start(), calls=%async_computation.6 | async-start | bytes 1048576 | tf_op jit(solution)/shard_map/psum | solution.py:27
  62.3 215.9 %collective-permute-start = (bf16[1,4,2,128,128]{4,3,2,1,0:T(8,128)(2,1)S(1)}, bf16[1,4,2,128,128]{4,3,2,1,0:T(8,128)(2,1)S(1)}, u32[]{:S(2)}, u32[]{:S(2)}) collective-permute-start(bf16[1,4,2,128,128]{4,3,2,1,0:T(8,128)(2,1)S(1)} %get-tuple-element.60), channel_id=1, source_target_pairs={{0,4},{4,8},{8,12},{12,16},{16,20},{20,24},{24,28},{28,32},{32,36}... | collective-permute-start | bytes 786440 | tf_op jit(solution)/shard_map/ppermute | solution.py:19
  64.0 215.7 %collective-permute-start.1 = (bf16[1,4,2,128,128]{4,3,2,1,0:T(8,128)(2,1)S(1)}, bf16[1,4,2,128,128]{4,3,2,1,0:T(8,128)(2,1)S(1)}, u32[]{:S(2)}, u32[]{:S(2)}) collective-permute-start(bf16[1,4,2,128,128]{4,3,2,1,0:T(8,128)(2,1)S(1)} %get-tuple-element.60), channel_id=1, source_target_pairs={{4,0},{8,4},{12,8},{16,12},{20,16},{24,20},{28,24},{32,28},{36,32}... | collective-permute-start | bytes 786440 | tf_op jit(solution)/shard_map/ppermute | solution.py:20
  287.5 6.7 %copy-start.4 = (bf16[1,4,8,1,128,128]{5,4,3,2,1,0:T(8,128)(2,1)}, bf16[1,4,8,1,128,128]{5,4,3,2,1,0:T(8,128)(2,1)S(1)}, u32[]{:S(2)}) copy-start(bf16[1,4,8,1,128,128]{5,4,3,2,1,0:T(8,128)(2,1)S(1)} %get-tuple-element.56) | copy-start | bytes 3145732
  287.9 2.0 copy-start.1
  300.4 1.6 copy-start.3
  303.5 1.9 copy-start
  305.4 1.3 copy-start.2
  320.7 203.2 %all-to-all-start.4 = ((bf16[128,2,128,128]{3,2,1,0:T(8,128)(2,1)}), bf16[128,2,128,128]{3,2,1,0:T(8,128)(2,1)}, u32[]{:S(2)}, u32[]{:S(2)}) async-start(bf16[128,2,128,128]{3,2,1,0:T(8,128)(2,1)} %select_select_fusion), calls=%async_computation.4 | async-start | bytes 16777216 | tf_op jit(solution)/shard_map/all_to_all | solution.py:39
  331.7 218.6 %all-reduce.4.cloned.1.call-start = ((), (), s32[]{:S(2)}) async-start(), calls=%async_computation.5 | async-start | bytes 2097152 | tf_op jit(solution)/shard_map/psum | solution.py:152
  335.5 201.1 %collective-permute-start.2 = (bf16[1,4,2,128,128]{4,1,3,2,0:T(4,128)(2,1)S(1)}, bf16[1,4,2,128,128]{4,1,3,2,0:T(4,128)(2,1)S(1)}, u32[]{:S(2)}, u32[]{:S(2)}) collective-permute-start(bf16[1,4,2,128,128]{4,1,3,2,0:T(4,128)(2,1)S(1)} %get-tuple-element.53), channel_id=1, source_target_pairs={{0,4},{4,8},{8,12},{12,16},{16,20},{20,24},{24,28},{28,32},{32,36}... | collective-permute-start | bytes 786440 | tf_op jit(solution)/shard_map/ppermute | solution.py:19
  337.2 199.4 %collective-permute-start.3 = (bf16[1,4,2,128,128]{4,1,3,2,0:T(4,128)(2,1)S(1)}, bf16[1,4,2,128,128]{4,1,3,2,0:T(4,128)(2,1)S(1)}, u32[]{:S(2)}, u32[]{:S(2)}) collective-permute-start(bf16[1,4,2,128,128]{4,1,3,2,0:T(4,128)(2,1)S(1)} %get-tuple-element.54), channel_id=1, source_target_pairs={{4,0},{8,4},{12,8},{16,12},{20,16},{24,20},{28,24},{32,28},{36,32}... | collective-permute-start | bytes 786440 | tf_op jit(solution)/shard_map/ppermute | solution.py:20
Sparse Core Ops, SparseCore 0:
  65.2 209.5 all-reduce.5
  335.9 214.3 all-reduce.3
where the time goes:
time: 568 us; the launch traced here: 565 us
  waiting for transfers between devices  414 us (73%)
  local copies, waits for them, and re-layouts  56.3 us (10%)
  starting transfers between devices  41.7 us (7%)
  other arithmetic  20.9 us (4%)
  matrix products  17.4 us (3%)
  between operations  14.3 us (3%)
    psum x1, waiting for transfers between devices, broadcast(): return lax.psum(block, axis)  211 us
    all_to_all x2, waiting for transfers between devices, trade(): lax.all_to_all(buffer, 'seq', split_axis=0, concat_axis=0, tiled=True)  185 us
    all_to_all x2, starting transfers between devices, trade(): lax.all_to_all(buffer, 'seq', split_axis=0, concat_axis=0, tiled=True)  25.4 us
    psum x1, waiting for transfers between devices, on_device(): global_total = lax.psum(global_part, 'seq')  13.7 us
    all_to_all x1, local copies, waits for them, and re-layouts, trade(): lax.all_to_all(buffer, 'seq', split_axis=0, concat_axis=0, tiled=True)  12.7 us
    unnamed x22, local copies, waits for them, and re-layouts  11.6 us
  transfers between devices with their start and end apart: 11, of which 4 were waited for; matrix products, arithmetic and copies ran while one was open for 8% of the time, Pallas kernels for 0%

commit v1 on v0

v1 whole, which is shorter than its diff:
```python
import math

import jax
import jax.numpy as jnp
from jax import lax
from jax.experimental import pallas as pl
from jax.experimental.pallas import tpu as pltpu
from jax.sharding import PartitionSpec as P

HD = 128
BLK = 128
NX = 4
NZ = 8
NY = 4
PAIR = 2 * HD
COL = 2 * NZ
ROW = 2 * NX
SCALE = 1.0 / math.sqrt(HD)
NEG = -1e30
MESH = pl.DeviceIdType.MESH
NT = (((1,), (1,)), ((), ()))
NN = (((1,), (0,)), ((), ()))
TN = (((0,), (0,)), ((), ()))


def dot(a, b, dims):
    return lax.dot_general(a, b, dims, preferred_element_type=jnp.float32)


def position():
    s = lax.axis_index("seq")
    y = lax.axis_index("head")
    x = s // (2 * NZ)
    z = (s // 2) % NZ
    c = s % 2
    return x, z, c, y


def place_of(x, z, c):
    return (x * NZ + z) * 2 + c


def remote(src, dst, send_sem, recv_sem, dev):
    return pltpu.make_async_remote_copy(
        src_ref=src, dst_ref=dst, send_sem=send_sem, recv_sem=recv_sem,
        device_id=dev, device_id_type=MESH,
    )


def meet(devs):
    barrier = pltpu.get_barrier_semaphore()
    for dev in devs:
        pl.semaphore_signal(barrier, inc=1, device_id=dev, device_id_type=MESH)
    pl.semaphore_wait(barrier, len(devs))


def unit_slots(xr, cb, x, z, c, h, rb_ref):
    xq = (x + xr) % NX
    block = COL * xq + 2 * z + cb
    base = ((2 * c + h) * (NX * COL) + block) * 3
    slots = []
    for r in range(3):
        j = rb_ref[base + r] - COL * x
        here = (j >= 0) & (j < COL)
        slots.append((jnp.clip(j, 0, COL - 1), jnp.where(here, 0.0, NEG)))
    edge = (x == 0) | (x == NX - 1)
    slots.append((jnp.where(x == NX - 1, COL - 1, 0), jnp.where(edge, 0.0, NEG)))
    if xr == 0:
        slots.append((2 * z, None))
        slots.append((2 * z + 1, None))
    if cb == 0 and xr in (0, 1):
        ok = (z != 0) if xr == 0 else (z == 0)
        slots.append(((2 * z + COL - 1) % COL, jnp.where(ok, 0.0, NEG)))
    if cb == 1 and xr in (0, NX - 1):
        ok = (z != NZ - 1) if xr == 0 else (z == NZ - 1)
        slots.append(((2 * z + 2) % COL, jnp.where(ok, 0.0, NEG)))
    return xq, slots


def gather_kernel(rb_ref, q_ref, k_ref, v_ref, g_ref, kall, vall, qrow, grow, stats,
                  a_send, a_recv, a_own, g_send, g_recv, z_send, z_recv, x_send, x_recv, s_send, s_recv):
    x, z, c, y = position()
    me = y * 2 + c

    def member(d):
        other = (me + d) % (2 * NY)
        return other % 2, other // 2

    def at(xx, zz):
        return (place_of(xx, zz, c), y)

    group = []
    for d in range(1, 2 * NY):
        cc, yy = member(d)
        group.append((place_of(x, z, cc), yy))
    zdev = (at(x, (z + 1) % NZ), at(x, (z + NZ - 1) % NZ))
    xdev = [at((x + d) % NX, z) for d in range(1, NX)]
    partner = (place_of(x, z, 1 - c), y)
    meet(group + list(zdev) + xdev)

    def cols(cc, yy):
        return pl.ds(pl.multiple_of((yy * 2 + cc) * PAIR, PAIR), PAIR)

    rows = pl.ds(pl.multiple_of(y * 32, 32), 32)
    ins = (k_ref, v_ref, q_ref)
    bufs = (kall, vall, qrow)
    slot = (2 * z, 2 * z, 2 * x)
    sends = []
    own = []
    for t in range(3):
        dst = bufs[t].at[slot[t] + c, rows, :]
        for d in range(1, 2 * NY):
            cc, yy = member(d)
            cp = remote(ins[t].at[:, cols(cc, yy)], dst, a_send.at[t, d], a_recv.at[t, d], group[d - 1])
            cp.start()
            sends.append(cp)
        cp = pltpu.make_async_copy(ins[t].at[:, cols(c, y)], dst, a_own.at[t])
        cp.start()
        own.append(cp)
        if t == 1:
            gs = remote(g_ref.at[:, pl.ds(pl.multiple_of((1 - c) * PAIR, PAIR), PAIR)], grow.at[2 * x + c],
                        g_send, g_recv, partner)
            gs.start()
            sends.append(gs)
            go = pltpu.make_async_copy(g_ref.at[:, pl.ds(pl.multiple_of(c * PAIR, PAIR), PAIR)],
                                       grow.at[2 * x + c], a_own.at[3])
            go.start()

    def arrived(t):
        own[t].wait()
        for d in range(1, 2 * NY):
            other = (me + 2 * NY - d) % (2 * NY)
            cs, ys = other % 2, other // 2
            dst = bufs[t].at[slot[t] + cs, pl.ds(pl.multiple_of(ys * 32, 32), 32), :]
            remote(dst, dst, a_send.at[t, d], a_recv.at[t, d], partner).wait_recv()

    def zpiece(t, owner):
        return (kall, vall)[t].at[pl.ds(2 * owner, 2)]

    def zcopy(direction, step, t):
        owner = (z - step + NZ) % NZ if direction == 0 else (z + step) % NZ
        ref = zpiece(t, owner)
        return remote(ref, ref, z_send.at[direction, step, t], z_recv.at[direction, step, t], zdev[direction])

    def zwait(direction, step, t):
        owner = (z - 1 - step + NZ) % NZ if direction == 0 else (z + 1 + step) % NZ
        ref = zpiece(t, owner)
        remote(ref, ref, z_send.at[direction, step, t], z_recv.at[direction, step, t], zdev[direction]).wait_recv()

    def xpiece(t, owner):
        return (qrow, grow)[t].at[pl.ds(2 * owner, 2)]

    def xcopy(direction, step, t):
        owner = (x - step + NX) % NX if direction == 0 else (x + step) % NX
        ref = xpiece(t, owner)
        return remote(ref, ref, x_send.at[direction, step, t], x_recv.at[direction, step, t],
                      xdev[0] if direction == 0 else xdev[NX - 2])

    def xwait(direction, step, t):
        owner = (x - 1 - step + NX) % NX if direction == 0 else (x + 1 + step) % NX
        ref = xpiece(t, owner)
        remote(ref, ref, x_send.at[direction, step, t], x_recv.at[direction, step, t], xdev[0]).wait_recv()

    def go_on(cp):
        cp.start()
        sends.append(cp)

    for t in range(2):
        arrived(t)
        for direction in range(2):
            go_on(zcopy(direction, 0, t))
    go.wait()
    remote(grow.at[2 * x + 1 - c], grow.at[2 * x + 1 - c], g_send, g_recv, partner).wait_recv()
    for direction in range(2):
        go_on(xcopy(direction, 0, 1))
    arrived(2)
    for direction in range(2):
        go_on(xcopy(direction, 0, 0))
    last = NZ // 2 - 1
    for step in range(last):
        for t in range(2):
            for direction in range(2):
                zwait(direction, step, t)
                if step + 1 < last or direction == t:
                    go_on(zcopy(direction, step + 1, t))
        if step == 0:
            for t in (1, 0):
                for direction in range(2):
                    xwait(direction, 0, t)
                    if direction == t:
                        go_on(xcopy(direction, 1, t))
    for t in range(2):
        xwait(t, 1, t)
    for t in range(2):
        zwait(t, last, t)

    def one_head(h, carry):
        lanes = pl.ds(pl.multiple_of(h * HD, HD), HD)
        for xr in range(NX):
            for cb in range(2):
                xq, slots = unit_slots(xr, cb, x, z, c, h, rb_ref)
                q = qrow[2 * xq + cb, :, lanes]
                g = grow[2 * xq + cb, :, lanes]
                scores = []
                for j, bias in slots:
                    sc = dot(kall[j, :, lanes], q, NT) * SCALE
                    scores.append(sc if bias is None else sc + bias)
                peak = scores[0]
                for sc in scores[1:]:
                    peak = jnp.maximum(peak, sc)
                peak = jnp.max(peak, axis=0, keepdims=True)
                total = None
                weighted = None
                for (j, _), sc in zip(slots, scores):
                    e = jnp.exp(sc - peak)
                    w = e * dot(vall[j, :, lanes], g, NT)
                    total = e if total is None else total + e
                    weighted = w if weighted is None else weighted + w
                u = h * ROW + 2 * xq + cb
                stats[x, 0, pl.ds(u, 1), :] = peak
                stats[x, 1, pl.ds(u, 1), :] = jnp.sum(total, axis=0, keepdims=True)
                stats[x, 2, pl.ds(u, 1), :] = jnp.sum(weighted, axis=0, keepdims=True)
        return carry

    lax.fori_loop(0, 2, one_head, 0)
    for d in range(1, NX):
        go_on(remote(stats.at[x], stats.at[x], s_send.at[d], s_recv.at[d], xdev[d - 1]))
    for d in range(1, NX):
        src = (x + NX - d) % NX
        remote(stats.at[src], stats.at[src], s_send.at[d], s_recv.at[d], xdev[d - 1]).wait_recv()
    for cp in sends:
        cp.wait_send()


def grad_kernel(rb_ref, kall, vall, qrow, grow, stats, dk_ref, dv_ref, o_ref, dq_ref, dk_acc, dv_acc):
    x, z, c, y = position()
    dk_acc[...] = jnp.zeros_like(dk_acc)
    dv_acc[...] = jnp.zeros_like(dv_acc)

    def one_head(h, carry):
        lanes = pl.ds(pl.multiple_of(h * HD, HD), HD)
        for xr in range(NX):
            for cb in range(2):
                xq, slots = unit_slots(xr, cb, x, z, c, h, rb_ref)
                u = h * ROW + 2 * xq + cb
                peaks = [stats[i, 0, pl.ds(u, 1), :] for i in range(NX)]
                peak = jnp.maximum(jnp.maximum(peaks[0], peaks[1]), jnp.maximum(peaks[2], peaks[3]))
                shift = [jnp.exp(p - peak) for p in peaks]
                total = sum(stats[i, 1, pl.ds(u, 1), :] * shift[i] for i in range(NX))
                delta = sum(stats[i, 2, pl.ds(u, 1), :] * shift[i] for i in range(NX))
                inverse = 1.0 / total
                delta = delta * inverse
                q = qrow[2 * xq + cb, :, lanes]
                g = grow[2 * xq + cb, :, lanes]
                out = None
                dq = None
                for j, bias in slots:
                    k = kall[j, :, lanes]
                    v = vall[j, :, lanes]
                    sc = dot(k, q, NT) * SCALE
                    if bias is not None:
                        sc = sc + bias
                    w = jnp.exp(sc - peak) * inverse
                    wb = w.astype(jnp.bfloat16)
                    ds = (w * (dot(v, g, NT) - delta)).astype(jnp.bfloat16)
                    dv_acc[j, :, lanes] += dot(wb, g, NN)
                    dk_acc[j, :, lanes] += dot(ds, q, NN)
                    o1 = dot(wb, v, TN)
                    q1 = dot(ds, k, TN)
                    out = o1 if out is None else out + o1
                    dq = q1 if dq is None else dq + q1
                o_ref[2 * xq + cb, :, lanes] = out.astype(jnp.bfloat16)
                dq_ref[2 * xq + cb, :, lanes] = (dq * SCALE).astype(jnp.bfloat16)
        return carry

    lax.fori_loop(0, 2, one_head, 0)
    dk_ref[...] = (dk_acc[...] * SCALE).astype(jnp.bfloat16)
    dv_ref[...] = dv_acc[...].astype(jnp.bfloat16)


def reduce_kernel(dk, dv, o, dq, o_out, dq_out, dk_out, dv_out,
                  zin, zsum, xin, xsum, final, z_send, z_recv, x_send, x_recv, f_send, f_recv):
    x, z, c, y = position()

    def at(xx, zz):
        return (place_of(xx, zz, c), y)

    zdev = (at(x, (z + 1) % NZ), at(x, (z + NZ - 1) % NZ))
    xdev = (at((x + 1) % NX, z), at((x + NX - 1) % NX, z))
    partner = (place_of(x, z, 1 - c), y)
    meet(list(zdev) + list(xdev) + [partner])
    sends = []
    f32 = jnp.float32

    def go_on(cp):
        cp.start()
        sends.append(cp)

    def chain(parts, arrive, summed, ssem, rsem, devs, pos, count, half):
        steps = count // 2

        def target(direction, step):
            away = steps - step
            return (pos + away) % count if direction == 0 else (pos + count - away) % count

        def first(direction, t):
            return 0 if t == half[direction] else 1

        def send(direction, step, t):
            mine = parts[t].at[pl.ds(2 * target(direction, step), 2)]
            if step == first(direction, t):
                src = mine
            else:
                src = summed.at[direction, step, t]
                got = wait(direction, step - 1, t)
                src[...] = (got[...].astype(f32) + mine[...].astype(f32)).astype(jnp.bfloat16)
            go_on(remote(src, arrive.at[direction, step, t], ssem.at[direction, step, t],
                         rsem.at[direction, step, t], devs[direction]))

        def wait(direction, step, t):
            ref = arrive.at[direction, step, t]
            remote(ref, ref, ssem.at[direction, step, t], rsem.at[direction, step, t], devs[direction]).wait_recv()
            return ref

        return steps, first, send, wait

    zsteps, zfirst, zgo, zwait = chain((dk, dv), zin, zsum, z_send, z_recv, zdev, z, NZ, (0, 1))
    xsteps, xfirst, xgo, xwait = chain((o, dq), xin, xsum, x_send, x_recv, xdev, x, NX, (0, 1))

    def both(go, first, step):
        for late in (True, False):
            for direction in range(2):
                for t in range(2):
                    if step >= first(direction, t) and (first(direction, t) == 1) == late:
                        go(direction, step, t)

    both(zgo, zfirst, 0)
    both(xgo, xfirst, 0)
    for step in range(1, zsteps):
        both(zgo, zfirst, step)
        if step < xsteps:
            both(xgo, xfirst, step)

    outs = (o_out, dq_out, dk_out, dv_out)
    here = pl.ds(pl.multiple_of(c * PAIR, PAIR), PAIR)

    def finish(n, parts, t, pos, wait, steps):
        a = wait(0, steps - 1, t)
        b = wait(1, steps - 1, t)
        mine = parts[t].at[pl.ds(2 * pos, 2)]
        final[n] = (mine[1 - c].astype(f32) + a[1 - c].astype(f32) + b[1 - c].astype(f32)).astype(jnp.bfloat16)
        go_on(remote(final.at[n], outs[n].at[:, here], f_send.at[n], f_recv.at[n], partner))
        outs[n][:, here] = (mine[c].astype(f32) + a[c].astype(f32) + b[c].astype(f32)).astype(jnp.bfloat16)

    for t in range(2):
        finish(t, (o, dq), t, x, xwait, xsteps)
    for t in (1, 0):
        finish(2 + t, (dk, dv), t, z, zwait, zsteps)
    there = pl.ds(pl.multiple_of((1 - c) * PAIR, PAIR), PAIR)
    for n in (0, 1, 3, 2):
        remote(final.at[n], outs[n].at[:, there], f_send.at[n], f_recv.at[n], partner).wait_recv()
    for cp in sends:
        cp.wait_send()


def vmem():
    return pl.BlockSpec(memory_space=pltpu.VMEM)


def smem():
    return pl.BlockSpec(memory_space=pltpu.SMEM)


def on_device(query_rows, key_rows, value_rows, out_grad, random_blocks):
    bf16, f32 = jnp.bfloat16, jnp.float32
    dma = pltpu.SemaphoreType.DMA
    lists = random_blocks.reshape(-1)
    column = jax.ShapeDtypeStruct((COL, BLK, PAIR), bf16)
    row = jax.ShapeDtypeStruct((ROW, BLK, PAIR), bf16)
    gathered = pl.pallas_call(
        gather_kernel,
        out_shape=(column, column, row, row, jax.ShapeDtypeStruct((NX, 3, 2 * ROW, HD), f32)),
        in_specs=[smem()] + [vmem()] * 4,
        out_specs=[vmem()] * 5,
        scratch_shapes=[
            dma((3, 2 * NY)), dma((3, 2 * NY)), dma((4,)), dma, dma,
            dma((2, NZ // 2, 2)), dma((2, NZ // 2, 2)),
            dma((2, NX // 2, 2)), dma((2, NX // 2, 2)),
            dma((NX,)), dma((NX,)),
        ],
        compiler_params=pltpu.CompilerParams(collective_id=0, has_side_effects=True),
        name="gather",
    )(lists, query_rows, key_rows, value_rows, out_grad)
    parts = pl.pallas_call(
        grad_kernel,
        out_shape=(column, column, row, row),
        in_specs=[smem()] + [vmem()] * 5,
        out_specs=[vmem()] * 4,
        scratch_shapes=[pltpu.VMEM((COL, BLK, PAIR), f32)] * 2,
        name="grads",
    )(lists, *gathered)
    full = jax.ShapeDtypeStruct((BLK, 2 * PAIR), bf16)
    return pl.pallas_call(
        reduce_kernel,
        out_shape=(full,) * 4,
        in_specs=[vmem()] * 4,
        out_specs=[vmem()] * 4,
        scratch_shapes=[
            pltpu.VMEM((2, NZ // 2, 2, 2, BLK, PAIR), bf16), pltpu.VMEM((2, NZ // 2, 2, 2, BLK, PAIR), bf16),
            pltpu.VMEM((2, NX // 2, 2, 2, BLK, PAIR), bf16), pltpu.VMEM((2, NX // 2, 2, 2, BLK, PAIR), bf16),
            pltpu.VMEM((4, BLK, PAIR), bf16),
            dma((2, NZ // 2, 2)), dma((2, NZ // 2, 2)),
            dma((2, NX // 2, 2)), dma((2, NX // 2, 2)),
            dma((4,)), dma((4,)),
        ],
        compiler_params=pltpu.CompilerParams(collective_id=1, has_side_effects=True),
        name="reduce",
    )(*parts)


def solution(mesh):
    in_specs = (
        P(("seq", "head"), None),
        P(("seq", "head"), None),
        P(("seq", "head"), None),
        P("seq", "head"),
        P("head", None, None),
    )
    out_specs = (P("seq", "head"),) * 4
    return jax.shard_map(
        on_device, mesh=mesh, in_specs=in_specs, out_specs=out_specs, check_vma=False
    )
```

time: 568 us -> 106 us (0.19)
  waiting for transfers between devices: 414 us -> 0 us
  Pallas kernels: 0 us -> 99.1 us
  local copies, waits for them, and re-layouts: 56.3 us -> 5.76 us
  starting transfers between devices: 41.7 us -> 0 us
  other arithmetic: 20.9 us -> 0 us
  matrix products: 17.4 us -> 0 us
  between operations: 14.3 us -> 0.66 us
    psum x2 -> x0, waiting for transfers between devices: 224 us -> none  [the longest x1 211 us: broadcast(): return lax.psum(block, axis)]
    all_to_all x5 -> x0, waiting for transfers between devices: 189 us -> none  [the longest x2 185 us: trade(): lax.all_to_all(buffer, 'seq', split_axis=0, concat_axis=0, tiled=True)]
    pallas_call x0 -> x3, Pallas kernels: none -> 99.1 us  [the longest x1 47.6 us: on_device(): pl.pallas_call(gather_kernel, out_shape=(column, column, row, row, jax.Sh...]
    all_to_all x5 -> x0, starting transfers between devices: 38 us -> none  [the longest x2 25.4 us: trade(): lax.all_to_all(buffer, 'seq', split_axis=0, concat_axis=0, tiled=True)]
    dot_general x7 -> x0, matrix products: 17.4 us -> none  [the longest x1 6.01 us: on_device(): jnp.dot(targets.astype(jnp.bfloat16), returned.reshape(seq_count * capaci...]
    all_to_all x4 -> x0, local copies, waits for them, and re-layouts: 17.4 us -> none  [the longest x1 12.7 us: trade(): lax.all_to_all(buffer, 'seq', split_axis=0, concat_axis=0, tiled=True)]
    gather x3 -> x0, local copies, waits for them, and re-layouts: 16.6 us -> none  [the longest x1 6.28 us: on_device(): jnp.take(random_terms, back_index, axis=0)]
    select_n x5 -> x0, other arithmetic: 15.3 us -> none  [the longest x1 7.55 us: on_device(): jnp.where(back_valid[:, None, None, None], jnp.take(random_terms, back_in...]
  transfers between devices with their start and end apart: 11 -> 0, of which waited for: 4 -> 0; matrix products, arithmetic and copies ran while one was open for 8% -> 0% of each run, Pallas kernels for 0% -> 0%
where the time goes in v1:
time: 106 us
  Pallas kernels  99.1 us (93%)
  local copies, waits for them, and re-layouts  5.76 us (5%)
    pallas_call x1, Pallas kernels, on_device(): pl.pallas_call(gather_kernel, out_shape=(column, column, row, row, jax.Sh...  47.6 us
    pallas_call x1, Pallas kernels, on_device(): pl.pallas_call(reduce_kernel, out_shape=(full,) * 4, in_specs=[vmem()] *...  29.6 us
    pallas_call x1, Pallas kernels, on_device(): pl.pallas_call(grad_kernel, out_shape=(column, column, row, row), in_spec...  21.9 us
    unnamed x11, local copies, waits for them, and re-layouts  4.96 us

profile of v1, /device:TPU:1, one launch (start us, length us, event | category | flops | bytes accessed | tf_op | source)
XLA Modules:
  0.0 105.5 jit_solution(8514724472698344240)
XLA Ops:
  0.6 0.8 copy.9
  1.4 0.8 reshape.11.rb_ref
  2.2 47.6 %gather.1 = (bf16[16,128,256]{2,1,0:T(8,128)(2,1)}, bf16[16,128,256]{2,1,0:T(8,128)(2,1)}, bf16[8,128,256]{2,1,0:T(8,128)(2,1)}, bf16[8,128,256]{2,1,0:T(8,128)(2,1)}, f32[4,3,16,128]{3,2,1,0:T(8,128)}) custom-call(s32[768]{0:T(1024)} %reshape.11.rb_ref, bf16[32,2048]{1,0:T(8,128)(2,1)} %q_ref.1, bf16[32,2048]{1,0:T(8,128)(2,1)} %k_ref.1, ...), custom_call_target="tpu_custom_call" | custom-call | tf_op jit(solution)/shard_map/gather/pallas_call | solution.py:380
  49.8 21.9 %grads.1 = (bf16[16,128,256]{2,1,0:T(8,128)(2,1)}, bf16[16,128,256]{2,1,0:T(8,128)(2,1)}, bf16[8,128,256]{2,1,0:T(8,128)(2,1)}, bf16[8,128,256]{2,1,0:T(8,128)(2,1)}) custom-call(s32[768]{0:T(1024)} %reshape.11.rb_ref, bf16[16,128,256]{2,1,0:T(8,128)(2,1)} %get-tuple-element.13.kall, bf16[16,128,256]{2,1,0:T(8,128)(2,1)} %get-tuple-element.14.vall, ...), custom_call_target="tpu_custom_call" | custom-call | tf_op jit(solution)/shard_map/grads/pallas_call | solution.py:394
  71.8 29.6 %reduce.1 = (bf16[128,512]{1,0:T(8,128)(2,1)}, bf16[128,512]{1,0:T(8,128)(2,1)}, bf16[128,512]{1,0:T(8,128)(2,1)}, bf16[128,512]{1,0:T(8,128)(2,1)}) custom-call(bf16[16,128,256]{2,1,0:T(8,128)(2,1)} %get-tuple-element.18.dk, bf16[16,128,256]{2,1,0:T(8,128)(2,1)} %get-tuple-element.19.dv, bf16[8,128,256]{2,1,0:T(8,128)(2,1)} %get-tuple-element.20.o, ...), custom_call_target="tpu_custom_call" | custom-call | tf_op jit(solution)/shard_map/reduce/pallas_call | solution.py:403
  101.4 0.0 copy-start.2
  101.4 1.6 %copy.14 = bf16[128,512]{1,0:T(8,128)(2,1)} copy(bf16[128,512]{1,0:T(8,128)(2,1)} %get-tuple-element.26) | data formatting | bytes 262144
  103.0 0.0 copy-done.2
  103.0 0.0 copy-start.1
  103.0 0.7 copy.15
  103.6 0.3 copy-done.1
  103.9 0.0 copy-start
  103.9 0.7 copy.16
  104.6 0.3 copy-done
  104.9 0.7 copy.17
Async XLA Ops:
  101.4 1.6 %copy-start.2 = (bf16[128,512]{1,0:T(8,128)(2,1)S(1)}, bf16[128,512]{1,0:T(8,128)(2,1)}, u32[]{:S(2)}) copy-start(bf16[128,512]{1,0:T(8,128)(2,1)} %get-tuple-element.27) | copy-start | bytes 393220
  103.0 1.0 copy-start.1
  103.9 1.0 copy-start

commit v2 on v1

--- a/solution.py
+++ b/solution.py
@@ -17,6 +17,7 @@
 ROW = 2 * NX
 SCALE = 1.0 / math.sqrt(HD)
 NEG = -1e30
+GROUP = 4
 MESH = pl.DeviceIdType.MESH
 NT = (((1,), (1,)), ((), ()))
 NN = (((1,), (0,)), ((), ()))
@@ -57,10 +58,9 @@
 def unit_slots(xr, cb, x, z, c, h, rb_ref):
     xq = (x + xr) % NX
     block = COL * xq + 2 * z + cb
-    base = ((2 * c + h) * (NX * COL) + block) * 3
     slots = []
     for r in range(3):
-        j = rb_ref[base + r] - COL * x
+        j = rb_ref[r, 2 * c + h, block] - COL * x
         here = (j >= 0) & (j < COL)
         slots.append((jnp.clip(j, 0, COL - 1), jnp.where(here, 0.0, NEG)))
     edge = (x == 0) | (x == NX - 1)
@@ -232,50 +232,115 @@
         cp.wait_send()
 
 
-def grad_kernel(rb_ref, kall, vall, qrow, grow, stats, dk_ref, dv_ref, o_ref, dq_ref, dk_acc, dv_acc):
-    x, z, c, y = position()
-    dk_acc[...] = jnp.zeros_like(dk_acc)
-    dv_acc[...] = jnp.zeros_like(dv_acc)
-
-    def one_head(h, carry):
-        lanes = pl.ds(pl.multiple_of(h * HD, HD), HD)
-        for xr in range(NX):
-            for cb in range(2):
-                xq, slots = unit_slots(xr, cb, x, z, c, h, rb_ref)
-                u = h * ROW + 2 * xq + cb
-                peaks = [stats[i, 0, pl.ds(u, 1), :] for i in range(NX)]
-                peak = jnp.maximum(jnp.maximum(peaks[0], peaks[1]), jnp.maximum(peaks[2], peaks[3]))
-                shift = [jnp.exp(p - peak) for p in peaks]
-                total = sum(stats[i, 1, pl.ds(u, 1), :] * shift[i] for i in range(NX))
-                delta = sum(stats[i, 2, pl.ds(u, 1), :] * shift[i] for i in range(NX))
-                inverse = 1.0 / total
-                delta = delta * inverse
-                q = qrow[2 * xq + cb, :, lanes]
-                g = grow[2 * xq + cb, :, lanes]
-                out = None
-                dq = None
-                for j, bias in slots:
-                    k = kall[j, :, lanes]
-                    v = vall[j, :, lanes]
-                    sc = dot(k, q, NT) * SCALE
-                    if bias is not None:
-                        sc = sc + bias
-                    w = jnp.exp(sc - peak) * inverse
-                    wb = w.astype(jnp.bfloat16)
-                    ds = (w * (dot(v, g, NT) - delta)).astype(jnp.bfloat16)
-                    dv_acc[j, :, lanes] += dot(wb, g, NN)
-                    dk_acc[j, :, lanes] += dot(ds, q, NN)
-                    o1 = dot(wb, v, TN)
-                    q1 = dot(ds, k, TN)
-                    out = o1 if out is None else out + o1
-                    dq = q1 if dq is None else dq + q1
-                o_ref[2 * xq + cb, :, lanes] = out.astype(jnp.bfloat16)
-                dq_ref[2 * xq + cb, :, lanes] = (dq * SCALE).astype(jnp.bfloat16)
+def grad_kernel(rb_ref, kall, vall, qrow, grow, stats, dk_ref, dv_ref, o_ref, dq_ref,
+                dk_acc, dv_acc, o_acc, dq_acc, peak_ref, inv_ref, delta_ref, todo):
+    x, z, c, _ = position()
+    bf16 = jnp.bfloat16
+
+    peaks = [stats[i, 0] for i in range(NX)]
+    peak = jnp.maximum(jnp.maximum(peaks[0], peaks[1]), jnp.maximum(peaks[2], peaks[3]))
+    shift = [jnp.exp(p - peak) for p in peaks]
+    inverse = 1.0 / sum(stats[i, 1] * shift[i] for i in range(NX))
+    peak_ref[...] = peak
+    inv_ref[...] = inverse
+    delta_ref[...] = sum(stats[i, 2] * shift[i] for i in range(NX)) * inverse
+
+    for acc in (dk_acc, dv_acc, o_acc, dq_acc):
+        acc[...] = jnp.zeros_like(acc)
+
+    count = jnp.int32(0)
+    for h in range(2):
+        ql = 2 * ((x + jnp.where(z == 0, 1, 0)) % NX)
+        qr = 2 * ((x + jnp.where(z == NZ - 1, NX - 1, 0)) % NX) + 1
+        todo[count] = ((h * ROW + ql) * COL) + (2 * z + COL - 1) % COL
+        todo[count + 1] = ((h * ROW + qr) * COL) + (2 * z + 2) % COL
+        count = count + 2
+    for h in range(2):
+        for i in range(ROW):
+            for r in range(3):
+                j = rb_ref[r, 2 * c + h, COL * (i // 2) + 2 * z + i % 2] - COL * x
+                here = (j >= 0) & (j < COL)
+                todo[count] = (h * ROW + i) * COL + j
+                count = count + here.astype(jnp.int32)
+
+    def pair_grads(k, v, q, g, peak, inverse, delta, bias):
+        sc = dot(k, q, NT) * SCALE
+        w = jnp.exp(sc - peak) * inverse
+        if bias is not None:
+            w = w * bias
+        ds = (w * (dot(v, g, NT) - delta)).astype(bf16)
+        return w.astype(bf16), ds
+
+    @pl.when((x == 0) | (x == NX - 1))
+    def _():
+        j = jnp.where(x == 0, 0, COL - 1)
+        for h in range(2):
+            lanes = slice(h * HD, (h + 1) * HD)
+            k, v = kall[j, :, lanes], vall[j, :, lanes]
+            dk = dv = None
+            for i in range(0, ROW, 2):
+                u = h * ROW + i
+                rows = [jnp.concatenate([ref[u:u + 1, :], ref[u + 1:u + 2, :]], axis=1)
+                        for ref in (peak_ref, inv_ref, delta_ref)]
+                q = qrow[i:i + 2, :, lanes].reshape(2 * BLK, HD)
+                g = grow[i:i + 2, :, lanes].reshape(2 * BLK, HD)
+                wb, ds = pair_grads(k, v, q, g, *rows, None)
+                dv1, dk1 = dot(wb, g, NN), dot(ds, q, NN)
+                dv = dv1 if dv is None else dv + dv1
+                dk = dk1 if dk is None else dk + dk1
+                o_acc[i:i + 2, :, lanes] = dot(wb, v, TN).reshape(2, BLK, HD)
+                dq_acc[i:i + 2, :, lanes] = dot(ds, k, TN).reshape(2, BLK, HD)
+            dk_acc[j, :, lanes] = dk
+            dv_acc[j, :, lanes] = dv
+
+    for h in range(2):
+        lanes = slice(h * HD, (h + 1) * HD)
+        mine = pl.ds(2 * z, 2)
+        own = pl.ds(2 * x, 2)
+        k = kall[mine, :, lanes].reshape(2 * BLK, HD)
+        v = vall[mine, :, lanes].reshape(2 * BLK, HD)
+        q = qrow[own, :, lanes].reshape(2 * BLK, HD)
+        g = grow[own, :, lanes].reshape(2 * BLK, HD)
+        u = h * ROW + 2 * x
+        rows = [jnp.concatenate([ref[pl.ds(u, 1), :], ref[pl.ds(u + 1, 1), :]], axis=1)
+                for ref in (peak_ref, inv_ref, delta_ref)]
+        wb, ds = pair_grads(k, v, q, g, *rows, None)
+        dv_acc[mine, :, lanes] += dot(wb, g, NN).reshape(2, BLK, HD)
+        dk_acc[mine, :, lanes] += dot(ds, q, NN).reshape(2, BLK, HD)
+        o_acc[own, :, lanes] += dot(wb, v, TN).reshape(2, BLK, HD)
+        dq_acc[own, :, lanes] += dot(ds, k, TN).reshape(2, BLK, HD)
+
+    def group(n, carry):
+        done = []
+        for t in range(GROUP):
+            at = n * GROUP + t
+            good = at < count
+            code = jnp.where(good, todo[at], todo[0])
+            u, j = code // COL, code % COL
+            h, i = u // ROW, u % ROW
+            lanes = pl.ds(pl.multiple_of(h * HD, HD), HD)
+            k, v = kall[j, :, lanes], vall[j, :, lanes]
+            q, g = qrow[i, :, lanes], grow[i, :, lanes]
+            wb, ds = pair_grads(k, v, q, g, peak_ref[pl.ds(u, 1), :], inv_ref[pl.ds(u, 1), :],
+                                delta_ref[pl.ds(u, 1), :], jnp.where(good, 1.0, 0.0))
+            done.append((i, j, lanes, dot(wb, g, NN), dot(ds, q, NN), dot(wb, v, TN), dot(ds, k, TN)))
+        for i, j, lanes, dv, dk, o, dq in done:
+            dv_acc[j, :, lanes] += dv
+            dk_acc[j, :, lanes] += dk
+            o_acc[i, :, lanes] += o
+            dq_acc[i, :, lanes] += dq
         return carry
 
-    lax.fori_loop(0, 2, one_head, 0)
-    dk_ref[...] = (dk_acc[...] * SCALE).astype(jnp.bfloat16)
-    dv_ref[...] = dv_acc[...].astype(jnp.bfloat16)
+    lax.fori_loop(0, (count + GROUP - 1) // GROUP, group, 0)
+    dk_ref[...] = (dk_acc[...] * SCALE).astype(bf16)
+    dv_ref[...] = dv_acc[...].astype(bf16)
+    o_ref[...] = o_acc[...].astype(bf16)
+    dq_ref[...] = (dq_acc[...] * SCALE).astype(bf16)
+
+
+def place_kernel(*refs):
+    for n in range(4):
+        refs[4 + n][...] = refs[n][...]
 
 
 def reduce_kernel(dk, dv, o, dq, o_out, dq_out, dk_out, dv_out,
@@ -374,7 +439,7 @@
 def on_device(query_rows, key_rows, value_rows, out_grad, random_blocks):
     bf16, f32 = jnp.bfloat16, jnp.float32
     dma = pltpu.SemaphoreType.DMA
-    lists = random_blocks.reshape(-1)
+    lists = random_blocks.transpose(2, 0, 1)
     column = jax.ShapeDtypeStruct((COL, BLK, PAIR), bf16)
     row = jax.ShapeDtypeStruct((ROW, BLK, PAIR), bf16)
     gathered = pl.pallas_call(
@@ -396,11 +461,12 @@
         out_shape=(column, column, row, row),
         in_specs=[smem()] + [vmem()] * 5,
         out_specs=[vmem()] * 4,
-        scratch_shapes=[pltpu.VMEM((COL, BLK, PAIR), f32)] * 2,
+        scratch_shapes=[pltpu.VMEM((COL, BLK, PAIR), f32)] * 2 + [pltpu.VMEM((ROW, BLK, PAIR), f32)] * 2
+        + [pltpu.VMEM((2 * ROW, HD), f32)] * 3 + [pltpu.SMEM((6 * ROW + 16,), jnp.int32)],
         name="grads",
     )(lists, *gathered)
     full = jax.ShapeDtypeStruct((BLK, 2 * PAIR), bf16)
-    return pl.pallas_call(
+    outs = pl.pallas_call(
         reduce_kernel,
         out_shape=(full,) * 4,
         in_specs=[vmem()] * 4,
@@ -416,6 +482,13 @@
         compiler_params=pltpu.CompilerParams(collective_id=1, has_side_effects=True),
         name="reduce",
     )(*parts)
+    return pl.pallas_call(
+        place_kernel,
+        out_shape=(full,) * 4,
+        in_specs=[vmem()] * 4,
+        out_specs=[vmem()] * 4,
+        name="place",
+    )(*outs)
 
 
 def solution(mesh):

time: 106 us -> 92.8 us (0.88)
  Pallas kernels: 99.1 us -> 92 us
  local copies, waits for them, and re-layouts: 5.76 us -> 0 us
    pallas_call x1, Pallas kernels: 21.9 us -> 12.8 us  [on_device(): pl.pallas_call(grad_kernel, out_shape=(column, column, row, row), in_spec...]
    unnamed x11 -> x0, local copies, waits for them, and re-layouts: 4.96 us -> none
    pallas_call x0 -> x1, Pallas kernels: none -> 1.89 us  [on_device(): pl.pallas_call(place_kernel, out_shape=(full,) * 4, in_specs=[vmem()] * 4...]
where the time goes in v2:
time: 92.8 us; the launch traced here: 92.6 us
  Pallas kernels  92 us (99%)
    pallas_call x1, Pallas kernels, on_device(): pl.pallas_call(gather_kernel, out_shape=(column, column, row, row, jax.Sh...  47.7 us
    pallas_call x1, Pallas kernels, on_device(): pl.pallas_call(reduce_kernel, out_shape=(full,) * 4, in_specs=[vmem()] *...  29.6 us
    pallas_call x1, Pallas kernels, on_device(): pl.pallas_call(grad_kernel, out_shape=(column, column, row, row), in_spec...  12.8 us
    pallas_call x1, Pallas kernels, on_device(): pl.pallas_call(place_kernel, out_shape=(full,) * 4, in_specs=[vmem()] * 4...  1.89 us

profile of v2, /device:TPU:1, one launch (start us, length us, event | category | flops | bytes accessed | tf_op | source)
XLA Modules:
  0.0 92.6 jit_solution(9377309109820505797)
XLA Ops:
  0.6 47.7 %gather.1 = (bf16[16,128,256]{2,1,0:T(8,128)(2,1)}, bf16[16,128,256]{2,1,0:T(8,128)(2,1)}, bf16[8,128,256]{2,1,0:T(8,128)(2,1)}, bf16[8,128,256]{2,1,0:T(8,128)(2,1)}, f32[4,3,16,128]{3,2,1,0:T(8,128)}) custom-call(s32[3,4,64]{2,1,0:T(4,128)} %bitcast.1, bf16[32,2048]{1,0:T(8,128)(2,1)} %q_ref.1, bf16[32,2048]{1,0:T(8,128)(2,1)} %k_ref.1, ...), custom_call_target="tpu_custom_call" | custom-call | tf_op jit(solution)/shard_map/gather/pallas_call | solution.py:445
  48.4 12.8 %grads.1 = (bf16[16,128,256]{2,1,0:T(8,128)(2,1)}, bf16[16,128,256]{2,1,0:T(8,128)(2,1)}, bf16[8,128,256]{2,1,0:T(8,128)(2,1)}, bf16[8,128,256]{2,1,0:T(8,128)(2,1)}) custom-call(s32[3,4,64]{2,1,0:T(4,128)} %bitcast.2, bf16[16,128,256]{2,1,0:T(8,128)(2,1)} %get-tuple-element.17.kall, bf16[16,128,256]{2,1,0:T(8,128)(2,1)} %get-tuple-element.18.vall, ...), custom_call_target="tpu_custom_call" | custom-call | tf_op jit(solution)/shard_map/grads/pallas_call | solution.py:459
  61.2 29.6 %reduce.1 = (bf16[128,512]{1,0:T(8,128)(2,1)}, bf16[128,512]{1,0:T(8,128)(2,1)}, bf16[128,512]{1,0:T(8,128)(2,1)}, bf16[128,512]{1,0:T(8,128)(2,1)}) custom-call(bf16[16,128,256]{2,1,0:T(8,128)(2,1)} %get-tuple-element.22.dk, bf16[16,128,256]{2,1,0:T(8,128)(2,1)} %get-tuple-element.23.dv, bf16[8,128,256]{2,1,0:T(8,128)(2,1)} %get-tuple-element.24.o, ...), custom_call_target="tpu_custom_call" | custom-call | tf_op jit(solution)/shard_map/reduce/pallas_call | solution.py:469
  90.7 1.9 %place.1 = (bf16[128,512]{1,0:T(8,128)(2,1)}, bf16[128,512]{1,0:T(8,128)(2,1)}, bf16[128,512]{1,0:T(8,128)(2,1)}, bf16[128,512]{1,0:T(8,128)(2,1)}) custom-call(bf16[128,512]{1,0:T(8,128)(2,1)} %get-tuple-element.26.refs_0_, bf16[128,512]{1,0:T(8,128)(2,1)} %get-tuple-element.27.refs_1_, bf16[128,512]{1,0:T(8,128)(2,1)} %get-tuple-element.28.refs_2_, ...), custom_call_target="tpu_custom_call" | custom-call | tf_op jit(solution)/shard_map/place/pallas_call | solution.py:485

commit v3 on v0

v3 whole, which is shorter than its diff:
```python
import math

import jax
import jax.numpy as jnp
from jax import lax
from jax.experimental import pallas as pl
from jax.experimental.pallas import tpu as pltpu
from jax.sharding import PartitionSpec as P

HD = 128
BLK = 128
NX = 4
NZ = 8
NY = 4
COL = 2 * NZ
ROW = 2 * NX
RAND = 3
LEFT = RAND * ROW
RIGHT = LEFT + 1
WIDE = LEFT + 2
ENTRIES = LEFT + 3
SCALE = 1.0 / math.sqrt(HD)
NEG = -1e30
MESH = pl.DeviceIdType.MESH
NT = (((1,), (1,)), ((), ()))
NN = (((1,), (0,)), ((), ()))
TN = (((0,), (0,)), ((), ()))
F32 = jnp.float32
BF16 = jnp.bfloat16


def dot(a, b, dims):
    return lax.dot_general(a, b, dims, preferred_element_type=F32)


def place_of(x, z, c):
    return (x * NZ + z) * 2 + c


def remote(src, dst, send_sem, recv_sem, dev):
    return pltpu.make_async_remote_copy(
        src_ref=src, dst_ref=dst, send_sem=send_sem, recv_sem=recv_sem,
        device_id=dev, device_id_type=MESH,
    )


def meet(devs):
    barrier = pltpu.get_barrier_semaphore()
    for dev in devs:
        pl.semaphore_signal(barrier, inc=1, device_id=dev, device_id_type=MESH)
    pl.semaphore_wait(barrier, len(devs))


def attention_kernel(rb_ref, q_ref, k_ref, v_ref, g_ref, o_out, dq_out, dk_out, dv_out,
                     kall0, kall1, vall0, vall1, qrow0, qrow1, grow0, grow1, sets, stats, rows, acc, wide_acc, own_acc, o_acc, dq_acc,
                     zin, zsum, xin, xsum, final, owner_s, prev_s, last_s,
                     a_send, a_recv, a_own, g_send, g_recv, g_own, z_send, z_recv, x_send, x_recv, s_send, s_recv,
                     rz_send, rz_recv, rx_send, rx_recv, f_send, f_recv):
    s = lax.axis_index("seq")
    y = lax.axis_index("head")
    x = s // (2 * NZ)
    z = (s // 2) % NZ
    c = s % 2
    me = y * 2 + c
    kall, vall, qrow, grow = (kall0, kall1), (vall0, vall1), (qrow0, qrow1), (grow0, grow1)

    def member(d):
        other = (me + d) % (2 * NY)
        return other % 2, other // 2

    def at(xx, zz):
        return (place_of(xx, zz, c), y)

    group = []
    for d in range(1, 2 * NY):
        cc, yy = member(d)
        group.append((place_of(x, z, cc), yy))
    zdev = (at(x, (z + 1) % NZ), at(x, (z + NZ - 1) % NZ))
    xall = [at((x + d) % NX, z) for d in range(1, NX)]
    xdev = (xall[0], xall[NX - 2])
    partner = (place_of(x, z, 1 - c), y)
    meet(group + list(zdev) + xall)

    sends = []

    def go_on(cp):
        cp.start()
        sends.append(cp)

    def lanes_of(n):
        return pl.ds(pl.multiple_of(n * HD, HD), HD)

    ins = (k_ref, v_ref, q_ref)
    bufs = (kall, vall, qrow)
    slot = (2 * z, 2 * z, 2 * x)
    own = {}

    def exchange(h, t):
        dst = bufs[t][h].at[slot[t] + c, pl.ds(pl.multiple_of(y * 32, 32), 32), :]
        for d in range(1, 2 * NY):
            cc, yy = member(d)
            go_on(remote(ins[t].at[:, lanes_of(yy * 4 + cc * 2 + h)], dst, a_send.at[h, t, d], a_recv.at[h, t, d],
                         group[d - 1]))
        own[h, t] = pltpu.make_async_copy(ins[t].at[:, lanes_of(me * 2 + h)], dst, a_own.at[h, t])
        own[h, t].start()

    def exchange_grad(h):
        go_on(remote(g_ref.at[:, lanes_of(2 * (1 - c) + h)], grow[h].at[2 * x + c], g_send.at[h], g_recv.at[h], partner))
        own[h, 3] = pltpu.make_async_copy(g_ref.at[:, lanes_of(2 * c + h)], grow[h].at[2 * x + c], g_own.at[h])
        own[h, 3].start()

    def arrived(h, t):
        own[h, t].wait()
        for d in range(1, 2 * NY):
            other = (me + 2 * NY - d) % (2 * NY)
            cs, ys = other % 2, other // 2
            dst = bufs[t][h].at[slot[t] + cs, pl.ds(pl.multiple_of(ys * 32, 32), 32), :]
            remote(dst, dst, a_send.at[h, t, d], a_recv.at[h, t, d], partner).wait_recv()

    def arrived_grad(h):
        own[h, 3].wait()
        dst = grow[h].at[2 * x + 1 - c]
        remote(dst, dst, g_send.at[h], g_recv.at[h], partner).wait_recv()

    def ring(bufs2, send, recv, devs, pos, count):
        def piece(h, t, owner):
            return bufs2[t][h].at[pl.ds(2 * owner, 2)]

        def copy(h, direction, step, t):
            owner = (pos + count - step) % count if direction == 0 else (pos + step) % count
            ref = piece(h, t, owner)
            go_on(remote(ref, ref, send.at[h, direction, step, t], recv.at[h, direction, step, t], devs[direction]))

        def wait(h, direction, step, t):
            owner = (pos + count - 1 - step) % count if direction == 0 else (pos + 1 + step) % count
            ref = piece(h, t, owner)
            remote(ref, ref, send.at[h, direction, step, t], recv.at[h, direction, step, t],
                   devs[direction]).wait_recv()

        return copy, wait

    zcopy, zwait = ring((kall, vall), z_send, z_recv, zdev, z, NZ)
    xcopy, xwait = ring((qrow, grow), x_send, x_recv, xdev, x, NX)
    zlast = NZ // 2 - 1

    def zstart(h):
        for t in range(2):
            arrived(h, t)
            for direction in range(2):
                zcopy(h, direction, 0, t)

    def xstart(h):
        arrived_grad(h)
        for direction in range(2):
            xcopy(h, direction, 0, 1)
        arrived(h, 2)
        for direction in range(2):
            xcopy(h, direction, 0, 0)

    def zstep(h, step):
        for t in range(2):
            for direction in range(2):
                zwait(h, direction, step, t)
                if step + 1 < zlast or direction == t:
                    zcopy(h, direction, step + 1, t)

    def xstep(h):
        for t in (1, 0):
            for direction in range(2):
                xwait(h, direction, 0, t)
                if direction == t:
                    xcopy(h, direction, 1, t)

    def zend(h):
        for t in range(2):
            zwait(h, t, zlast, t)

    def xend(h):
        for t in range(2):
            xwait(h, t, 1, t)

    edge = (x == 0) | (x == NX - 1)
    wide_at = jnp.where(x == 0, 0, COL - 1)
    left_q = 2 * ((x + jnp.where(z == 0, 1, 0)) % NX)
    right_q = 2 * ((x + jnp.where(z == NZ - 1, NX - 1, 0)) % NX) + 1
    left_k = (2 * z + COL - 1) % COL
    right_k = (2 * z + 2) % COL

    def plan(h):
        owners = []
        for i in range(ROW):
            for r in range(RAND):
                j = rb_ref[r, 2 * c + h, COL * (i // 2) + 2 * z + i % 2] - COL * x
                owners.append(jnp.where((j >= 0) & (j < COL), j, -1))
        owners += [left_k, right_k, jnp.where(edge, wide_at, -1)]
        for e in range(ENTRIES):
            prev = jnp.int32(-1)
            for f in range(e):
                prev = jnp.where(owners[f] == owners[e], f, prev)
            owner_s[h * ENTRIES + e] = owners[e]
            prev_s[h * ENTRIES + e] = prev
        for j in range(COL):
            last = jnp.int32(-1)
            for e in range(ENTRIES):
                last = jnp.where(owners[e] == j, e, last)
            last_s[h * COL + j] = last

    def listed(h, e):
        j = owner_s[h * ENTRIES + e]
        return jnp.maximum(j, 0), jnp.where(j < 0, NEG, 0.0)

    wide_bias = jnp.where(edge, 0.0, NEG)

    def measure(ks, vs, q, g):
        scores = []
        for k, bias in ks:
            sc = dot(k, q, NT) * SCALE
            scores.append(sc if bias is None else sc + bias)
        peak = scores[0]
        for sc in scores[1:]:
            peak = jnp.maximum(peak, sc)
        peak = jnp.max(peak, axis=0, keepdims=True)
        total = weighted = None
        for v, sc in zip(vs, scores):
            e = jnp.exp(sc - peak)
            w = e * dot(v, g, NT)
            total = e if total is None else total + e
            weighted = w if weighted is None else weighted + w
        return peak, jnp.sum(total, axis=0, keepdims=True), jnp.sum(weighted, axis=0, keepdims=True)

    def window(h):
        mine = pl.ds(2 * z, 2)
        here = pl.ds(2 * x, 2)
        return tuple(ref[h][at_, :, :].reshape(2 * BLK, HD)
                     for ref, at_ in ((kall, mine), (vall, mine), (qrow, here), (grow, here)))

    def count_units(h, units):
        for i in units:
            ks, vs = [], []
            for r in range(RAND):
                j, bias = listed(h, RAND * i + r)
                ks.append((kall[h][j], bias))
                vs.append(vall[h][j])
            ks.append((kall[h][wide_at], wide_bias))
            vs.append(vall[h][wide_at])
            for n, row in enumerate(measure(ks, vs, qrow[h][i], grow[h][i])):
                sets[h, 0, n, i:i + 1, :] = row

    def count_rest(h):
        for part in range(1, 4):
            sets[h, part, 0] = jnp.full((ROW, HD), NEG, F32)
            sets[h, part, 1] = jnp.zeros((ROW, HD), F32)
            sets[h, part, 2] = jnp.zeros((ROW, HD), F32)
        k, v, q, g = window(h)
        for n, row in enumerate(measure([(k, None)], [v], q, g)):
            sets[h, 1, n, pl.ds(2 * x, 1), :] = row[:, :HD]
            sets[h, 1, n, pl.ds(2 * x + 1, 1), :] = row[:, HD:]
        for part, qi, kj in ((2, left_q, left_k), (3, right_q, right_k)):
            for n, row in enumerate(measure([(kall[h][kj], None)], [vall[h][kj]], qrow[h][qi], grow[h][qi])):
                sets[h, part, n, pl.ds(qi, 1), :] = row

    def merge(parts):
        peak = jnp.maximum(jnp.maximum(parts[0][0], parts[1][0]), jnp.maximum(parts[2][0], parts[3][0]))
        shift = [jnp.exp(p[0] - peak) for p in parts]
        total = sum(p[1] * f for p, f in zip(parts, shift))
        return peak, total, sum(p[2] * f for p, f in zip(parts, shift))

    def send_stats(h):
        for n, value in enumerate(merge([[sets[h, part, n] for n in range(3)] for part in range(4)])):
            stats[h, x, n] = value
        for d in range(1, NX):
            go_on(remote(stats.at[h, x], stats.at[h, x], s_send.at[h, d], s_recv.at[h, d], xall[d - 1]))

    def take_stats(h):
        for d in range(1, NX):
            src = (x + NX - d) % NX
            remote(stats.at[h, src], stats.at[h, src], s_send.at[h, d], s_recv.at[h, d], xall[d - 1]).wait_recv()
        peak, total, weighted = merge([[stats[h, i, n] for n in range(3)] for i in range(NX)])
        inverse = 1.0 / total
        rows[h, 0] = peak
        rows[h, 1] = inverse
        rows[h, 2] = weighted * inverse

    def weigh(k, v, q, g, row, bias):
        peak, inverse, delta = row
        sc = dot(k, q, NT) * SCALE
        if bias is not None:
            sc = sc + bias
        w = jnp.exp(sc - peak) * inverse
        return w.astype(BF16), (w * (dot(v, g, NT) - delta)).astype(BF16)

    def row_of(h, i):
        return [rows[h, n, pl.ds(i, 1), :] for n in range(3)]

    def store_entry(h, e, dk, dv):
        prev = prev_s[h * ENTRIES + e]
        back = jnp.maximum(prev, 0)
        acc[h, 0, e] = dk + jnp.where(prev < 0, 0.0, acc[h, 0, back])
        acc[h, 1, e] = dv + jnp.where(prev < 0, 0.0, acc[h, 1, back])

    def grad_units(h, units):
        for i in units:
            row = row_of(h, i)
            q, g = qrow[h][i], grow[h][i]
            o = dq = None
            for r in range(RAND + 1):
                if r < RAND:
                    j, bias = listed(h, RAND * i + r)
                else:
                    j, bias = wide_at, wide_bias
                k, v = kall[h][j], vall[h][j]
                wb, ds = weigh(k, v, q, g, row, bias)
                dk, dv = dot(ds, q, NN), dot(wb, g, NN)
                if r < RAND:
                    store_entry(h, RAND * i + r, dk, dv)
                elif i == 0:
                    wide_acc[h, 0] = dk
                    wide_acc[h, 1] = dv
                else:
                    wide_acc[h, 0] += dk
                    wide_acc[h, 1] += dv
                o1, q1 = dot(wb, v, TN), dot(ds, k, TN)
                o = o1 if o is None else o + o1
                dq = q1 if dq is None else dq + q1
            o_acc[h, i] = o
            dq_acc[h, i] = dq

    def grad_rim(h):
        for e, qi, kj in ((LEFT, left_q, left_k), (RIGHT, right_q, right_k)):
            k, v, q, g = kall[h][kj], vall[h][kj], qrow[h][qi], grow[h][qi]
            wb, ds = weigh(k, v, q, g, row_of(h, qi), None)
            store_entry(h, e, dot(ds, q, NN), dot(wb, g, NN))
            o_acc[h, qi] += dot(wb, v, TN)
            dq_acc[h, qi] += dot(ds, k, TN)
        store_entry(h, WIDE, wide_acc[h, 0], wide_acc[h, 1])

    def grad_own(h):
        k, v, q, g = window(h)
        row = [jnp.concatenate([a, b], axis=1) for a, b in zip(row_of(h, 2 * x), row_of(h, 2 * x + 1))]
        wb, ds = weigh(k, v, q, g, row, None)
        own_acc[h, 0] = dot(ds, q, NN).reshape(2, BLK, HD)
        own_acc[h, 1] = dot(wb, g, NN).reshape(2, BLK, HD)
        here = pl.ds(2 * x, 2)
        o_acc[h, here] += dot(wb, v, TN).reshape(2, BLK, HD)
        dq_acc[h, here] += dot(ds, k, TN).reshape(2, BLK, HD)

    def key_part(h, t, target):
        def one(b):
            last = last_s[h * COL + 2 * target + b]
            value = acc[h, t, jnp.maximum(last, 0)]
            value = jnp.where(last < 0, 0.0, value)
            return value * SCALE if t == 0 else value
        return one

    def query_part(h, t, target):
        def one(b):
            value = (o_acc, dq_acc)[t][h, 2 * target + b]
            return value * SCALE if t == 1 else value
        return one

    def summing(part, arrive, summed, send, recv, devs, pos, count):
        steps = count // 2

        def wait(h, direction, step, t):
            ref = arrive.at[h, direction, step, t]
            remote(ref, ref, send.at[h, direction, step, t], recv.at[h, direction, step, t],
                   devs[direction]).wait_recv()
            return ref

        def go(h, direction, step, t):
            away = steps - step
            target = (pos + away) % count if direction == 0 else (pos + count - away) % count
            mine = part(h, t, target)
            src = summed.at[h, direction, step, t]
            got = None if step == (0 if t == direction else 1) else wait(h, direction, step - 1, t)
            for b in range(2):
                value = mine(b)
                if got is not None:
                    value = value + got[b].astype(F32)
                src[b] = value.astype(BF16)
            go_on(remote(src, arrive.at[h, direction, step, t], send.at[h, direction, step, t],
                         recv.at[h, direction, step, t], devs[direction]))

        def begin(h):
            for direction in range(2):
                go(h, direction, 0, direction)
            for direction in range(2):
                go(h, direction, 1, 1 - direction)

        def step_on(h, step):
            for t in (1, 0):
                for direction in range(2):
                    if not (step == 1 and t != direction):
                        go(h, direction, step, t)

        return begin, step_on, lambda h, t: (wait(h, 0, steps - 1, t), wait(h, 1, steps - 1, t))

    zbegin, zsum_on, zfinal = summing(key_part, zin, zsum, rz_send, rz_recv, zdev, z, NZ)
    xbegin, xsum_on, xfinal = summing(query_part, xin, xsum, rx_send, rx_recv, xdev, x, NX)
    outs = (o_out, dq_out, dk_out, dv_out)

    def finish(h, n, got, mine, extra):
        def value(b):
            v = mine(b) + got[0][b].astype(F32) + got[1][b].astype(F32)
            return (v if extra is None else v + extra(b)).astype(BF16)
        lanes = lanes_of(2 * c + h)
        final[h, n] = value(1 - c)
        go_on(remote(final.at[h, n], outs[n].at[:, lanes], f_send.at[h, n], f_recv.at[h, n], partner))
        outs[n][:, lanes] = value(c)

    def finish_queries(h):
        for t in range(2):
            finish(h, t, xfinal(h, t), query_part(h, t, x), None)

    def finish_keys(h):
        for t in range(2):
            finish(h, 2 + t, zfinal(h, t), key_part(h, t, z),
                   lambda b, t=t: own_acc[h, t, b] * SCALE if t == 0 else own_acc[h, t, b])

    for h in range(2):
        exchange(h, 0)
        exchange(h, 1)
        exchange_grad(h)
        exchange(h, 2)
    plan(0)
    zstart(0)
    xstart(0)
    plan(1)
    zstep(0, 0)
    xstep(0)
    zstep(0, 1)
    zstep(0, 2)
    zstart(1)
    xstart(1)
    xend(0)
    zend(0)
    pairs = [(i, i + 1) for i in range(0, ROW, 2)]
    for units in pairs:
        count_units(0, units)
    count_rest(0)
    send_stats(0)
    zstep(1, 0)
    xstep(1)
    take_stats(0)
    grad_units(0, pairs[0])
    zstep(1, 1)
    grad_units(0, pairs[1])
    xend(1)
    grad_units(0, pairs[2])
    zstep(1, 2)
    grad_units(0, pairs[3])
    grad_rim(0)
    zbegin(0)
    xbegin(0)
    zend(1)
    for units in pairs:
        count_units(1, units)
    count_rest(1)
    send_stats(1)
    zsum_on(0, 1)
    xsum_on(0, 1)
    grad_own(0)
    zsum_on(0, 2)
    take_stats(1)
    grad_units(1, pairs[0])
    finish_queries(0)
    grad_units(1, pairs[1])
    zsum_on(0, 3)
    grad_units(1, pairs[2])
    grad_units(1, pairs[3])
    grad_rim(1)
    zbegin(1)
    xbegin(1)
    grad_own(1)
    finish_keys(0)
    zsum_on(1, 1)
    xsum_on(1, 1)
    zsum_on(1, 2)
    finish_queries(1)
    zsum_on(1, 3)
    finish_keys(1)
    for h in range(2):
        for n in range(4):
            dst = outs[n].at[:, lanes_of(2 * (1 - c) + h)]
            remote(final.at[h, n], dst, f_send.at[h, n], f_recv.at[h, n], partner).wait_recv()
    for cp in sends:
        cp.wait_send()


def place_kernel(*refs):
    for n in range(4):
        refs[4 + n][...] = refs[n][...]


def vmem():
    return pl.BlockSpec(memory_space=pltpu.VMEM)


def smem():
    return pl.BlockSpec(memory_space=pltpu.SMEM)


def on_device(query_rows, key_rows, value_rows, out_grad, random_blocks):
    dma = pltpu.SemaphoreType.DMA
    mem = pltpu.VMEM
    tile = (BLK, HD)
    full = jax.ShapeDtypeStruct((BLK, 4 * HD), BF16)
    zs, xs = NZ // 2, NX // 2
    outs = pl.pallas_call(
        attention_kernel,
        out_shape=(full,) * 4,
        in_specs=[smem()] + [vmem()] * 4,
        out_specs=[vmem()] * 4,
        scratch_shapes=[
            *[mem((COL,) + tile, BF16)] * 4, *[mem((ROW,) + tile, BF16)] * 4,
            mem((2, 4, 3, ROW, HD), F32), mem((2, NX, 3, ROW, HD), F32), mem((2, 3, ROW, HD), F32),
            mem((2, 2, ENTRIES) + tile, F32), mem((2, 2) + tile, F32), mem((2, 2, 2) + tile, F32),
            mem((2, ROW) + tile, F32), mem((2, ROW) + tile, F32),
            mem((2, 2, zs, 2, 2) + tile, BF16), mem((2, 2, zs, 2, 2) + tile, BF16),
            mem((2, 2, xs, 2, 2) + tile, BF16), mem((2, 2, xs, 2, 2) + tile, BF16),
            mem((2, 4) + tile, BF16),
            pltpu.SMEM((2 * ENTRIES,), jnp.int32), pltpu.SMEM((2 * ENTRIES,), jnp.int32), pltpu.SMEM((2 * COL,), jnp.int32),
            dma((2, 3, 2 * NY)), dma((2, 3, 2 * NY)), dma((2, 3)), dma((2,)), dma((2,)), dma((2,)),
            dma((2, 2, zs, 2)), dma((2, 2, zs, 2)), dma((2, 2, xs, 2)), dma((2, 2, xs, 2)),
            dma((2, NX)), dma((2, NX)),
            dma((2, 2, zs, 2)), dma((2, 2, zs, 2)), dma((2, 2, xs, 2)), dma((2, 2, xs, 2)),
            dma((2, 4)), dma((2, 4)),
        ],
        compiler_params=pltpu.CompilerParams(collective_id=0, has_side_effects=True),
        name="attention",
    )(random_blocks.transpose(2, 0, 1), query_rows, key_rows, value_rows, out_grad)
    return pl.pallas_call(
        place_kernel,
        out_shape=(full,) * 4,
        in_specs=[vmem()] * 4,
        out_specs=[vmem()] * 4,
        name="place",
    )(*outs)


def solution(mesh):
    in_specs = (
        P(("seq", "head"), None),
        P(("seq", "head"), None),
        P(("seq", "head"), None),
        P("seq", "head"),
        P("head", None, None),
    )
    out_specs = (P("seq", "head"),) * 4
    return jax.shard_map(
        on_device, mesh=mesh, in_specs=in_specs, out_specs=out_specs, check_vma=False
    )
```

time: 568 us -> 86 us (0.15)
  waiting for transfers between devices: 414 us -> 0 us
  Pallas kernels: 0 us -> 85.3 us
  local copies, waits for them, and re-layouts: 56.3 us -> 0 us
  starting transfers between devices: 41.7 us -> 0 us
  other arithmetic: 20.9 us -> 0 us
  matrix products: 17.4 us -> 0 us
  between operations: 14.3 us -> 0.64 us
    psum x2 -> x0, waiting for transfers between devices: 224 us -> none  [the longest x1 211 us: broadcast(): return lax.psum(block, axis)]
    all_to_all x5 -> x0, waiting for transfers between devices: 189 us -> none  [the longest x2 185 us: trade(): lax.all_to_all(buffer, 'seq', split_axis=0, concat_axis=0, tiled=True)]
    pallas_call x0 -> x2, Pallas kernels: none -> 85.3 us  [the longest x1 83.4 us: on_device(): pl.pallas_call(attention_kernel, out_shape=(full,) * 4, in_specs=[smem()]...]
    all_to_all x5 -> x0, starting transfers between devices: 38 us -> none  [the longest x2 25.4 us: trade(): lax.all_to_all(buffer, 'seq', split_axis=0, concat_axis=0, tiled=True)]
    dot_general x7 -> x0, matrix products: 17.4 us -> none  [the longest x1 6.01 us: on_device(): jnp.dot(targets.astype(jnp.bfloat16), returned.reshape(seq_count * capaci...]
    all_to_all x4 -> x0, local copies, waits for them, and re-layouts: 17.4 us -> none  [the longest x1 12.7 us: trade(): lax.all_to_all(buffer, 'seq', split_axis=0, concat_axis=0, tiled=True)]
    gather x3 -> x0, local copies, waits for them, and re-layouts: 16.6 us -> none  [the longest x1 6.28 us: on_device(): jnp.take(random_terms, back_index, axis=0)]
    select_n x5 -> x0, other arithmetic: 15.3 us -> none  [the longest x1 7.55 us: on_device(): jnp.where(back_valid[:, None, None, None], jnp.take(random_terms, back_in...]
  transfers between devices with their start and end apart: 11 -> 0, of which waited for: 4 -> 0; matrix products, arithmetic and copies ran while one was open for 8% -> 0% of each run, Pallas kernels for 0% -> 0%
where the time goes in v3:
time: 86 us; the launch traced here: 85.9 us
  Pallas kernels  85.3 us (99%)
    pallas_call x1, Pallas kernels, on_device(): pl.pallas_call(attention_kernel, out_shape=(full,) * 4, in_specs=[smem()]...  83.4 us
    pallas_call x1, Pallas kernels, on_device(): pl.pallas_call(place_kernel, out_shape=(full,) * 4, in_specs=[vmem()] * 4...  1.89 us

profile of v3, /device:TPU:1, one launch (start us, length us, event | category | flops | bytes accessed | tf_op | source)
XLA Modules:
  0.0 85.9 jit_solution(17705327633347611441)
XLA Ops:
  0.6 83.4 %attention.1 = (bf16[128,512]{1,0:T(8,128)(2,1)}, bf16[128,512]{1,0:T(8,128)(2,1)}, bf16[128,512]{1,0:T(8,128)(2,1)}, bf16[128,512]{1,0:T(8,128)(2,1)}) custom-call(s32[3,4,64]{2,1,0:T(4,128)} %bitcast.1, bf16[32,2048]{1,0:T(8,128)(2,1)} %q_ref.1, bf16[32,2048]{1,0:T(8,128)(2,1)} %k_ref.1, bf16[32,2048]{1,0:T(8,128)(2,1)} %v_ref.1, bf16[128,512]{1,0:T(8,128)(2,1)} %g_ref.1), custom_call_target="tpu_custom_call" | custom-call | tf_op jit(solution)/shard_map/attention/pallas_call | solution.py:509
  84.0 1.9 %place.1 = (bf16[128,512]{1,0:T(8,128)(2,1)}, bf16[128,512]{1,0:T(8,128)(2,1)}, bf16[128,512]{1,0:T(8,128)(2,1)}, bf16[128,512]{1,0:T(8,128)(2,1)}) custom-call(bf16[128,512]{1,0:T(8,128)(2,1)} %get-tuple-element.8.refs_0_, bf16[128,512]{1,0:T(8,128)(2,1)} %get-tuple-element.9.refs_1_, bf16[128,512]{1,0:T(8,128)(2,1)} %get-tuple-element.10.refs_2_, ...), custom_call_target="tpu_custom_call" | custom-call | tf_op jit(solution)/shard_map/place/pallas_call | solution.py:532

commit v4 on v3

--- a/solution.py
+++ b/solution.py
@@ -143,11 +143,10 @@
     xcopy, xwait = ring((qrow, grow), x_send, x_recv, xdev, x, NX)
     zlast = NZ // 2 - 1
 
-    def zstart(h):
-        for t in range(2):
-            arrived(h, t)
-            for direction in range(2):
-                zcopy(h, direction, 0, t)
+    def zstart(h, t):
+        arrived(h, t)
+        for direction in range(2):
+            zcopy(h, direction, 0, t)
 
     def xstart(h):
         arrived_grad(h)
@@ -157,8 +156,8 @@
         for direction in range(2):
             xcopy(h, direction, 0, 0)
 
-    def zstep(h, step):
-        for t in range(2):
+    def zstep(h, step, tensors=(0, 1)):
+        for t in tensors:
             for direction in range(2):
                 zwait(h, direction, step, t)
                 if step + 1 < zlast or direction == t:
@@ -211,19 +210,27 @@
 
     wide_bias = jnp.where(edge, 0.0, NEG)
 
+    def stack(tiles):
+        return tiles[0] if len(tiles) == 1 else jnp.concatenate(tiles, axis=0)
+
+    def pieces(value, count):
+        size = value.shape[0] // count
+        return [value[n * size:(n + 1) * size] for n in range(count)]
+
+    def score(ks, q):
+        scores = pieces(dot(stack([k for k, _ in ks]), q, NT), len(ks))
+        return [sc * SCALE if bias is None else sc * SCALE + bias for sc, (_, bias) in zip(scores, ks)]
+
     def measure(ks, vs, q, g):
-        scores = []
-        for k, bias in ks:
-            sc = dot(k, q, NT) * SCALE
-            scores.append(sc if bias is None else sc + bias)
+        scores = score(ks, q)
         peak = scores[0]
         for sc in scores[1:]:
             peak = jnp.maximum(peak, sc)
         peak = jnp.max(peak, axis=0, keepdims=True)
         total = weighted = None
-        for v, sc in zip(vs, scores):
+        for sc, dp in zip(scores, pieces(dot(stack(vs), g, NT), len(vs))):
             e = jnp.exp(sc - peak)
-            w = e * dot(v, g, NT)
+            w = e * dp
             total = e if total is None else total + e
             weighted = w if weighted is None else weighted + w
         return peak, jnp.sum(total, axis=0, keepdims=True), jnp.sum(weighted, axis=0, keepdims=True)
@@ -234,15 +241,19 @@
         return tuple(ref[h][at_, :, :].reshape(2 * BLK, HD)
                      for ref, at_ in ((kall, mine), (vall, mine), (qrow, here), (grow, here)))
 
+    def tiles_of(h, i):
+        ks, vs = [], []
+        for r in range(RAND):
+            j, bias = listed(h, RAND * i + r)
+            ks.append((kall[h][j], bias))
+            vs.append(vall[h][j])
+        ks.append((kall[h][wide_at], wide_bias))
+        vs.append(vall[h][wide_at])
+        return ks, vs
+
     def count_units(h, units):
         for i in units:
-            ks, vs = [], []
-            for r in range(RAND):
-                j, bias = listed(h, RAND * i + r)
-                ks.append((kall[h][j], bias))
-                vs.append(vall[h][j])
-            ks.append((kall[h][wide_at], wide_bias))
-            vs.append(vall[h][wide_at])
+            ks, vs = tiles_of(h, i)
             for n, row in enumerate(measure(ks, vs, qrow[h][i], grow[h][i])):
                 sets[h, 0, n, i:i + 1, :] = row
 
@@ -281,13 +292,16 @@
         rows[h, 1] = inverse
         rows[h, 2] = weighted * inverse
 
-    def weigh(k, v, q, g, row, bias):
+    def weigh(ks, vs, q, g, row):
         peak, inverse, delta = row
-        sc = dot(k, q, NT) * SCALE
-        if bias is not None:
-            sc = sc + bias
-        w = jnp.exp(sc - peak) * inverse
-        return w.astype(BF16), (w * (dot(v, g, NT) - delta)).astype(BF16)
+        wb, ds = [], []
+        for sc, dp in zip(score(ks, q), pieces(dot(stack(vs), g, NT), len(vs))):
+            w = jnp.exp(sc - peak) * inverse
+            wb.append(w.astype(BF16))
+            ds.append((w * (dp - delta)).astype(BF16))
+        wb, ds = stack(wb), stack(ds)
+        k, v = stack([k for k, _ in ks]), stack(vs)
+        return dot(ds, q, NN), dot(wb, g, NN), dot(wb, v, TN), dot(ds, k, TN)
 
     def row_of(h, i):
         return [rows[h, n, pl.ds(i, 1), :] for n in range(3)]
@@ -300,17 +314,9 @@
 
     def grad_units(h, units):
         for i in units:
-            row = row_of(h, i)
-            q, g = qrow[h][i], grow[h][i]
-            o = dq = None
-            for r in range(RAND + 1):
-                if r < RAND:
-                    j, bias = listed(h, RAND * i + r)
-                else:
-                    j, bias = wide_at, wide_bias
-                k, v = kall[h][j], vall[h][j]
-                wb, ds = weigh(k, v, q, g, row, bias)
-                dk, dv = dot(ds, q, NN), dot(wb, g, NN)
+            ks, vs = tiles_of(h, i)
+            dks, dvs, o, dq = weigh(ks, vs, qrow[h][i], grow[h][i], row_of(h, i))
+            for r, (dk, dv) in enumerate(zip(pieces(dks, len(ks)), pieces(dvs, len(vs)))):
                 if r < RAND:
                     store_entry(h, RAND * i + r, dk, dv)
                 elif i == 0:
@@ -319,30 +325,26 @@
                 else:
                     wide_acc[h, 0] += dk
                     wide_acc[h, 1] += dv
-                o1, q1 = dot(wb, v, TN), dot(ds, k, TN)
-                o = o1 if o is None else o + o1
-                dq = q1 if dq is None else dq + q1
             o_acc[h, i] = o
             dq_acc[h, i] = dq
 
     def grad_rim(h):
         for e, qi, kj in ((LEFT, left_q, left_k), (RIGHT, right_q, right_k)):
-            k, v, q, g = kall[h][kj], vall[h][kj], qrow[h][qi], grow[h][qi]
-            wb, ds = weigh(k, v, q, g, row_of(h, qi), None)
-            store_entry(h, e, dot(ds, q, NN), dot(wb, g, NN))
-            o_acc[h, qi] += dot(wb, v, TN)
-            dq_acc[h, qi] += dot(ds, k, TN)
+            dk, dv, o, dq = weigh([(kall[h][kj], None)], [vall[h][kj]], qrow[h][qi], grow[h][qi], row_of(h, qi))
+            store_entry(h, e, dk, dv)
+            o_acc[h, qi] += o
+            dq_acc[h, qi] += dq
         store_entry(h, WIDE, wide_acc[h, 0], wide_acc[h, 1])
 
     def grad_own(h):
         k, v, q, g = window(h)
         row = [jnp.concatenate([a, b], axis=1) for a, b in zip(row_of(h, 2 * x), row_of(h, 2 * x + 1))]
-        wb, ds = weigh(k, v, q, g, row, None)
-        own_acc[h, 0] = dot(ds, q, NN).reshape(2, BLK, HD)
-        own_acc[h, 1] = dot(wb, g, NN).reshape(2, BLK, HD)
+        dk, dv, o, dq = weigh([(k, None)], [v], q, g, row)
+        own_acc[h, 0] = dk.reshape(2, BLK, HD)
+        own_acc[h, 1] = dv.reshape(2, BLK, HD)
         here = pl.ds(2 * x, 2)
-        o_acc[h, here] += dot(wb, v, TN).reshape(2, BLK, HD)
-        dq_acc[h, here] += dot(ds, k, TN).reshape(2, BLK, HD)
+        o_acc[h, here] += o.reshape(2, BLK, HD)
+        dq_acc[h, here] += dq.reshape(2, BLK, HD)
 
     def key_part(h, t, target):
         def one(b):
@@ -417,37 +419,44 @@
             finish(h, 2 + t, zfinal(h, t), key_part(h, t, z),
                    lambda b, t=t: own_acc[h, t, b] * SCALE if t == 0 else own_acc[h, t, b])
 
+    exchange(0, 0)
+    exchange(0, 1)
+    exchange(1, 0)
+    exchange(1, 1)
     for h in range(2):
-        exchange(h, 0)
-        exchange(h, 1)
         exchange_grad(h)
         exchange(h, 2)
+    zstart(0, 0)
+    zstart(0, 1)
+    zstart(1, 0)
+    zstep(0, 0)
+    zstart(1, 1)
+    xstart(0)
     plan(0)
-    zstart(0)
-    xstart(0)
+    zstep(0, 1)
+    zstep(1, 0, (0,))
+    xstart(1)
+    xstep(0)
+    zstep(0, 2)
+    zstep(1, 0, (1,))
     plan(1)
-    zstep(0, 0)
-    xstep(0)
-    zstep(0, 1)
-    zstep(0, 2)
-    zstart(1)
-    xstart(1)
     xend(0)
     zend(0)
     pairs = [(i, i + 1) for i in range(0, ROW, 2)]
-    for units in pairs:
-        count_units(0, units)
+    count_units(0, pairs[0])
+    count_units(0, pairs[1])
+    zstep(1, 1)
+    count_units(0, pairs[2])
+    count_units(0, pairs[3])
     count_rest(0)
     send_stats(0)
-    zstep(1, 0)
     xstep(1)
+    zstep(1, 2)
     take_stats(0)
     grad_units(0, pairs[0])
-    zstep(1, 1)
     grad_units(0, pairs[1])
     xend(1)
     grad_units(0, pairs[2])
-    zstep(1, 2)
     grad_units(0, pairs[3])
     grad_rim(0)
     zbegin(0)

time: 86 us -> 79.5 us (0.924)
  Pallas kernels: 85.3 us -> 78.8 us
    pallas_call x1, Pallas kernels: 83.4 us -> 76.9 us  [on_device(): pl.pallas_call(attention_kernel, out_shape=(full,) * 4, in_specs=[smem()]...]
where the time goes in v4:
time: 79.5 us; the launch traced here: 79.4 us
  Pallas kernels  78.8 us (99%)
    pallas_call x1, Pallas kernels, on_device(): pl.pallas_call(attention_kernel, out_shape=(full,) * 4, in_specs=[smem()]...  76.9 us
    pallas_call x1, Pallas kernels, on_device(): pl.pallas_call(place_kernel, out_shape=(full,) * 4, in_specs=[vmem()] * 4...  1.89 us

profile of v4, /device:TPU:1, one launch (start us, length us, event | category | flops | bytes accessed | tf_op | source)
XLA Modules:
  0.0 79.4 jit_solution(446824567757788743)
XLA Ops:
  0.6 76.9 %attention.1 = (bf16[128,512]{1,0:T(8,128)(2,1)}, bf16[128,512]{1,0:T(8,128)(2,1)}, bf16[128,512]{1,0:T(8,128)(2,1)}, bf16[128,512]{1,0:T(8,128)(2,1)}) custom-call(s32[3,4,64]{2,1,0:T(4,128)} %bitcast.1, bf16[32,2048]{1,0:T(8,128)(2,1)} %q_ref.1, bf16[32,2048]{1,0:T(8,128)(2,1)} %k_ref.1, bf16[32,2048]{1,0:T(8,128)(2,1)} %v_ref.1, bf16[128,512]{1,0:T(8,128)(2,1)} %g_ref.1), custom_call_target="tpu_custom_call" | custom-call | tf_op jit(solution)/shard_map/attention/pallas_call | solution.py:518
  77.5 1.9 %place.1 = (bf16[128,512]{1,0:T(8,128)(2,1)}, bf16[128,512]{1,0:T(8,128)(2,1)}, bf16[128,512]{1,0:T(8,128)(2,1)}, bf16[128,512]{1,0:T(8,128)(2,1)}) custom-call(bf16[128,512]{1,0:T(8,128)(2,1)} %get-tuple-element.8.refs_0_, bf16[128,512]{1,0:T(8,128)(2,1)} %get-tuple-element.9.refs_1_, bf16[128,512]{1,0:T(8,128)(2,1)} %get-tuple-element.10.refs_2_, ...), custom_call_target="tpu_custom_call" | custom-call | tf_op jit(solution)/shard_map/place/pallas_call | solution.py:541

commit v5 on v4

--- a/solution.py
+++ b/solution.py
@@ -53,9 +53,9 @@
 
 def attention_kernel(rb_ref, q_ref, k_ref, v_ref, g_ref, o_out, dq_out, dk_out, dv_out,
                      kall0, kall1, vall0, vall1, qrow0, qrow1, grow0, grow1, sets, stats, rows, acc, wide_acc, own_acc, o_acc, dq_acc,
-                     zin, zsum, xin, xsum, final, owner_s, prev_s, last_s,
+                     zin, zsum, xin, xsum, zfin, xfin, final, gift, owner_s, prev_s, last_s,
                      a_send, a_recv, a_own, g_send, g_recv, g_own, z_send, z_recv, x_send, x_recv, s_send, s_recv,
-                     rz_send, rz_recv, rx_send, rx_recv, f_send, f_recv):
+                     rz_send, rz_recv, rx_send, rx_recv, lz_send, lz_recv, lx_send, lx_recv, f_send, f_recv):
     s = lax.axis_index("seq")
     y = lax.axis_index("head")
     x = s // (2 * NZ)
@@ -79,7 +79,17 @@
     xall = [at((x + d) % NX, z) for d in range(1, NX)]
     xdev = (xall[0], xall[NX - 2])
     partner = (place_of(x, z, 1 - c), y)
-    meet(group + list(zdev) + xall)
+
+    def either(xx, zz):
+        return [(place_of(xx, zz, b), y) for b in range(2)]
+
+    def across(xx, zz):
+        return (place_of(xx, zz, 1 - c), y)
+
+    zcores = (either(x, (z + 1) % NZ), either(x, (z + NZ - 1) % NZ))
+    xcores = (either((x + 1) % NX, z), either((x + NX - 1) % NX, z))
+    meet(group + list(zdev) + xall + [across(x, (z + 1) % NZ), across(x, (z + NZ - 1) % NZ),
+                                      across((x + 1) % NX, z), across((x + NX - 1) % NX, z)])
 
     sends = []
 
@@ -360,12 +370,12 @@
             return value * SCALE if t == 1 else value
         return one
 
-    def summing(part, arrive, summed, send, recv, devs, pos, count):
+    def summing(part, arrive, summed, send, recv, devs, last, last_send, last_recv, cores, pos, count):
         steps = count // 2
 
-        def wait(h, direction, step, t):
-            ref = arrive.at[h, direction, step, t]
-            remote(ref, ref, send.at[h, direction, step, t], recv.at[h, direction, step, t],
+        def wait(h, direction, step, t, b):
+            ref = arrive.at[h, direction, step, t, b]
+            remote(ref, ref, send.at[h, direction, step, t, b], recv.at[h, direction, step, t, b],
                    devs[direction]).wait_recv()
             return ref
 
@@ -373,15 +383,18 @@
             away = steps - step
             target = (pos + away) % count if direction == 0 else (pos + count - away) % count
             mine = part(h, t, target)
-            src = summed.at[h, direction, step, t]
-            got = None if step == (0 if t == direction else 1) else wait(h, direction, step - 1, t)
             for b in range(2):
                 value = mine(b)
-                if got is not None:
-                    value = value + got[b].astype(F32)
-                src[b] = value.astype(BF16)
-            go_on(remote(src, arrive.at[h, direction, step, t], send.at[h, direction, step, t],
-                         recv.at[h, direction, step, t], devs[direction]))
+                if step != (0 if t == direction else 1):
+                    value = value + wait(h, direction, step - 1, t, b)[...].astype(F32)
+                src = summed.at[h, direction, step, t, b]
+                src[...] = value.astype(BF16)
+                if step == steps - 1:
+                    go_on(remote(src, last.at[h, t, c, direction], last_send.at[h, direction, t, b],
+                                 last_recv.at[h, direction, t, c], cores[direction][b]))
+                else:
+                    go_on(remote(src, arrive.at[h, direction, step, t, b], send.at[h, direction, step, t, b],
+                                 recv.at[h, direction, step, t, b], devs[direction]))
 
         def begin(h):
             for direction in range(2):
@@ -395,40 +408,52 @@
                     if not (step == 1 and t != direction):
                         go(h, direction, step, t)
 
-        return begin, step_on, lambda h, t: (wait(h, 0, steps - 1, t), wait(h, 1, steps - 1, t))
-
-    zbegin, zsum_on, zfinal = summing(key_part, zin, zsum, rz_send, rz_recv, zdev, z, NZ)
-    xbegin, xsum_on, xfinal = summing(query_part, xin, xsum, rx_send, rx_recv, xdev, x, NX)
+        def ended(h, t, core):
+            total = None
+            for direction in range(2):
+                ref = last.at[h, t, core, direction]
+                remote(ref, ref, last_send.at[h, direction, t, 0], last_recv.at[h, direction, t, core],
+                       partner).wait_recv()
+                total = ref[...].astype(F32) if total is None else total + ref[...].astype(F32)
+            return total
+
+        return begin, step_on, ended
+
+    zbegin, zsum_on, zended = summing(key_part, zin, zsum, rz_send, rz_recv, zdev, zfin, lz_send, lz_recv, zcores, z, NZ)
+    xbegin, xsum_on, xended = summing(query_part, xin, xsum, rx_send, rx_recv, xdev, xfin, lx_send, lx_recv, xcores, x, NX)
     outs = (o_out, dq_out, dk_out, dv_out)
 
-    def finish(h, n, got, mine, extra):
-        def value(b):
-            v = mine(b) + got[0][b].astype(F32) + got[1][b].astype(F32)
-            return (v if extra is None else v + extra(b)).astype(BF16)
-        lanes = lanes_of(2 * c + h)
-        final[h, n] = value(1 - c)
-        go_on(remote(final.at[h, n], outs[n].at[:, lanes], f_send.at[h, n], f_recv.at[h, n], partner))
-        outs[n][:, lanes] = value(c)
-
-    def finish_queries(h):
-        for t in range(2):
-            finish(h, t, xfinal(h, t), query_part(h, t, x), None)
-
-    def finish_keys(h):
-        for t in range(2):
-            finish(h, 2 + t, zfinal(h, t), key_part(h, t, z),
-                   lambda b, t=t: own_acc[h, t, b] * SCALE if t == 0 else own_acc[h, t, b])
+    def own_part(h, n, b):
+        if n < 2:
+            return query_part(h, n, x)(b)
+        value = own_acc[h, n - 2, b]
+        return key_part(h, n - 2, z)(b) + (value * SCALE if n == 2 else value)
+
+    def give(h, ns):
+        for n in ns:
+            final[h, n] = own_part(h, n, 1 - c).astype(BF16)
+            go_on(remote(final.at[h, n], gift.at[h, n], f_send.at[h, n], f_recv.at[h, n], partner))
+
+    def finish(h, ns):
+        for n in ns:
+            ended = xended if n < 2 else zended
+            mine = own_part(h, n, c) + ended(h, n % 2, c)
+            outs[n][:, lanes_of(2 * c + h)] = mine.astype(BF16)
+            remote(gift.at[h, n], gift.at[h, n], f_send.at[h, n], f_recv.at[h, n], partner).wait_recv()
+            theirs = gift[h, n].astype(F32) + ended(h, n % 2, 1 - c)
+            outs[n][:, lanes_of(2 * (1 - c) + h)] = theirs.astype(BF16)
 
     exchange(0, 0)
     exchange(0, 1)
     exchange(1, 0)
+    zstart(0, 0)
     exchange(1, 1)
-    for h in range(2):
-        exchange_grad(h)
-        exchange(h, 2)
-    zstart(0, 0)
     zstart(0, 1)
+    exchange_grad(0)
+    exchange(0, 2)
     zstart(1, 0)
+    exchange_grad(1)
+    exchange(1, 2)
     zstep(0, 0)
     zstart(1, 1)
     xstart(0)
@@ -454,44 +479,42 @@
     zstep(1, 2)
     take_stats(0)
     grad_units(0, pairs[0])
+    xend(1)
     grad_units(0, pairs[1])
-    xend(1)
     grad_units(0, pairs[2])
-    grad_units(0, pairs[3])
-    grad_rim(0)
-    zbegin(0)
-    xbegin(0)
     zend(1)
     for units in pairs:
         count_units(1, units)
     count_rest(1)
     send_stats(1)
+    grad_units(0, pairs[3])
+    grad_rim(0)
+    zbegin(0)
+    xbegin(0)
+    grad_own(0)
+    give(0, range(4))
+    take_stats(1)
+    grad_units(1, pairs[0])
     zsum_on(0, 1)
     xsum_on(0, 1)
-    grad_own(0)
+    grad_units(1, pairs[1])
+    grad_units(1, pairs[2])
     zsum_on(0, 2)
-    take_stats(1)
-    grad_units(1, pairs[0])
-    finish_queries(0)
-    grad_units(1, pairs[1])
-    zsum_on(0, 3)
-    grad_units(1, pairs[2])
     grad_units(1, pairs[3])
     grad_rim(1)
     zbegin(1)
     xbegin(1)
+    zsum_on(0, 3)
     grad_own(1)
-    finish_keys(0)
+    give(1, range(4))
     zsum_on(1, 1)
     xsum_on(1, 1)
+    finish(0, (0, 1))
     zsum_on(1, 2)
-    finish_queries(1)
+    finish(0, (2, 3))
+    finish(1, (0, 1))
     zsum_on(1, 3)
-    finish_keys(1)
-    for h in range(2):
-        for n in range(4):
-            dst = outs[n].at[:, lanes_of(2 * (1 - c) + h)]
-            remote(final.at[h, n], dst, f_send.at[h, n], f_recv.at[h, n], partner).wait_recv()
+    finish(1, (3, 2))
     for cp in sends:
         cp.wait_send()
 
@@ -527,12 +550,14 @@
             mem((2, ROW) + tile, F32), mem((2, ROW) + tile, F32),
             mem((2, 2, zs, 2, 2) + tile, BF16), mem((2, 2, zs, 2, 2) + tile, BF16),
             mem((2, 2, xs, 2, 2) + tile, BF16), mem((2, 2, xs, 2, 2) + tile, BF16),
-            mem((2, 4) + tile, BF16),
+            mem((2, 2, 2, 2) + tile, BF16), mem((2, 2, 2, 2) + tile, BF16),
+            mem((2, 4) + tile, BF16), mem((2, 4) + tile, BF16),
             pltpu.SMEM((2 * ENTRIES,), jnp.int32), pltpu.SMEM((2 * ENTRIES,), jnp.int32), pltpu.SMEM((2 * COL,), jnp.int32),
             dma((2, 3, 2 * NY)), dma((2, 3, 2 * NY)), dma((2, 3)), dma((2,)), dma((2,)), dma((2,)),
             dma((2, 2, zs, 2)), dma((2, 2, zs, 2)), dma((2, 2, xs, 2)), dma((2, 2, xs, 2)),
             dma((2, NX)), dma((2, NX)),
-            dma((2, 2, zs, 2)), dma((2, 2, zs, 2)), dma((2, 2, xs, 2)), dma((2, 2, xs, 2)),
+            dma((2, 2, zs, 2, 2)), dma((2, 2, zs, 2, 2)), dma((2, 2, xs, 2, 2)), dma((2, 2, xs, 2, 2)),
+            dma((2, 2, 2, 2)), dma((2, 2, 2, 2)), dma((2, 2, 2, 2)), dma((2, 2, 2, 2)),
             dma((2, 4)), dma((2, 4)),
         ],
         compiler_params=pltpu.CompilerParams(collective_id=0, has_side_effects=True),

time: 79.5 us -> 76.9 us (0.967)
  Pallas kernels: 78.8 us -> 76.2 us
    pallas_call x1, Pallas kernels: 76.9 us -> 74.3 us  [on_device(): pl.pallas_call(attention_kernel, out_shape=(full,) * 4, in_specs=[smem()]...]
where the time goes in v5:
time: 76.9 us; the launch traced here: 76.8 us
  Pallas kernels  76.2 us (99%)
    pallas_call x1, Pallas kernels, on_device(): pl.pallas_call(attention_kernel, out_shape=(full,) * 4, in_specs=[smem()]...  74.3 us
    pallas_call x1, Pallas kernels, on_device(): pl.pallas_call(place_kernel, out_shape=(full,) * 4, in_specs=[vmem()] * 4...  1.89 us

profile of v5, /device:TPU:1, one launch (start us, length us, event | category | flops | bytes accessed | tf_op | source)
XLA Modules:
  0.0 76.8 jit_solution(4840318325366505501)
XLA Ops:
  0.6 74.3 %attention.1 = (bf16[128,512]{1,0:T(8,128)(2,1)}, bf16[128,512]{1,0:T(8,128)(2,1)}, bf16[128,512]{1,0:T(8,128)(2,1)}, bf16[128,512]{1,0:T(8,128)(2,1)}) custom-call(s32[3,4,64]{2,1,0:T(4,128)} %bitcast.1, bf16[32,2048]{1,0:T(8,128)(2,1)} %q_ref.1, bf16[32,2048]{1,0:T(8,128)(2,1)} %k_ref.1, bf16[32,2048]{1,0:T(8,128)(2,1)} %v_ref.1, bf16[128,512]{1,0:T(8,128)(2,1)} %g_ref.1), custom_call_target="tpu_custom_call" | custom-call | tf_op jit(solution)/shard_map/attention/pallas_call | solution.py:541
  74.9 1.9 %place.1 = (bf16[128,512]{1,0:T(8,128)(2,1)}, bf16[128,512]{1,0:T(8,128)(2,1)}, bf16[128,512]{1,0:T(8,128)(2,1)}, bf16[128,512]{1,0:T(8,128)(2,1)}) custom-call(bf16[128,512]{1,0:T(8,128)(2,1)} %get-tuple-element.8.refs_0_, bf16[128,512]{1,0:T(8,128)(2,1)} %get-tuple-element.9.refs_1_, bf16[128,512]{1,0:T(8,128)(2,1)} %get-tuple-element.10.refs_2_, ...), custom_call_target="tpu_custom_call" | custom-call | tf_op jit(solution)/shard_map/place/pallas_call | solution.py:566

commit v6 on v5

--- a/solution.py
+++ b/solution.py
@@ -21,6 +21,7 @@
 ENTRIES = LEFT + 3
 SCALE = 1.0 / math.sqrt(HD)
 NEG = -1e30
+VMEM_LIMIT = 32 << 20
 MESH = pl.DeviceIdType.MESH
 NT = (((1,), (1,)), ((), ()))
 NN = (((1,), (0,)), ((), ()))
@@ -51,9 +52,9 @@
     pl.semaphore_wait(barrier, len(devs))
 
 
-def attention_kernel(rb_ref, q_ref, k_ref, v_ref, g_ref, o_out, dq_out, dk_out, dv_out,
+def attention_kernel(rb_in, q_ref, k_ref, v_ref, g_ref, o_out, dq_out, dk_out, dv_out,
                      kall0, kall1, vall0, vall1, qrow0, qrow1, grow0, grow1, sets, stats, rows, acc, wide_acc, own_acc, o_acc, dq_acc,
-                     zin, zsum, xin, xsum, zfin, xfin, final, gift, owner_s, prev_s, last_s,
+                     zin, zsum, xin, xsum, zfin, xfin, final, gift, rb_ref, owner_s, prev_s, last_s, rb_sem,
                      a_send, a_recv, a_own, g_send, g_recv, g_own, z_send, z_recv, x_send, x_recv, s_send, s_recv,
                      rz_send, rz_recv, rx_send, rx_recv, lz_send, lz_recv, lx_send, lx_recv, f_send, f_recv):
     s = lax.axis_index("seq")
@@ -91,6 +92,8 @@
     meet(group + list(zdev) + xall + [across(x, (z + 1) % NZ), across(x, (z + NZ - 1) % NZ),
                                       across((x + 1) % NX, z), across((x + NX - 1) % NX, z)])
 
+    lists = pltpu.make_async_copy(rb_in, rb_ref, rb_sem)
+    lists.start()
     sends = []
 
     def go_on(cp):
@@ -457,6 +460,7 @@
     zstep(0, 0)
     zstart(1, 1)
     xstart(0)
+    lists.wait()
     plan(0)
     zstep(0, 1)
     zstep(1, 0, (0,))
@@ -541,7 +545,7 @@
     outs = pl.pallas_call(
         attention_kernel,
         out_shape=(full,) * 4,
-        in_specs=[smem()] + [vmem()] * 4,
+        in_specs=[pl.BlockSpec(memory_space=pltpu.HBM)] * 5,
         out_specs=[vmem()] * 4,
         scratch_shapes=[
             *[mem((COL,) + tile, BF16)] * 4, *[mem((ROW,) + tile, BF16)] * 4,
@@ -552,7 +556,8 @@
             mem((2, 2, xs, 2, 2) + tile, BF16), mem((2, 2, xs, 2, 2) + tile, BF16),
             mem((2, 2, 2, 2) + tile, BF16), mem((2, 2, 2, 2) + tile, BF16),
             mem((2, 4) + tile, BF16), mem((2, 4) + tile, BF16),
-            pltpu.SMEM((2 * ENTRIES,), jnp.int32), pltpu.SMEM((2 * ENTRIES,), jnp.int32), pltpu.SMEM((2 * COL,), jnp.int32),
+            pltpu.SMEM((RAND, 4, NX * COL), jnp.int32),
+            pltpu.SMEM((2 * ENTRIES,), jnp.int32), pltpu.SMEM((2 * ENTRIES,), jnp.int32), pltpu.SMEM((2 * COL,), jnp.int32), dma,
             dma((2, 3, 2 * NY)), dma((2, 3, 2 * NY)), dma((2, 3)), dma((2,)), dma((2,)), dma((2,)),
             dma((2, 2, zs, 2)), dma((2, 2, zs, 2)), dma((2, 2, xs, 2)), dma((2, 2, xs, 2)),
             dma((2, NX)), dma((2, NX)),
@@ -560,14 +565,16 @@
             dma((2, 2, 2, 2)), dma((2, 2, 2, 2)), dma((2, 2, 2, 2)), dma((2, 2, 2, 2)),
             dma((2, 4)), dma((2, 4)),
         ],
-        compiler_params=pltpu.CompilerParams(collective_id=0, has_side_effects=True),
+        compiler_params=pltpu.CompilerParams(collective_id=0, has_side_effects=True, vmem_limit_bytes=VMEM_LIMIT),
         name="attention",
-    )(random_blocks.transpose(2, 0, 1), query_rows, key_rows, value_rows, out_grad)
+    )(*(pltpu.with_memory_space_constraint(a, pltpu.HBM)
+        for a in (random_blocks.transpose(2, 0, 1), query_rows, key_rows, value_rows, out_grad)))
     return pl.pallas_call(
         place_kernel,
         out_shape=(full,) * 4,
         in_specs=[vmem()] * 4,
         out_specs=[vmem()] * 4,
+        compiler_params=pltpu.CompilerParams(vmem_limit_bytes=4 << 20),
         name="place",
     )(*outs)
 

time: 76.9 us -> 74.2 us (0.965)
  Pallas kernels: 76.2 us -> 73.4 us
    pallas_call x1, Pallas kernels: 74.3 us -> 72.6 us  [on_device(): pl.pallas_call(attention_kernel, out_shape=(full,) * 4, in_specs=[pl.Bloc...]
    pallas_call x1, Pallas kernels: 1.89 us -> 0.82 us  [on_device(): pl.pallas_call(place_kernel, out_shape=(full,) * 4, in_specs=[vmem()] * 4...]
where the time goes in v6:
time: 74.2 us; the launch traced here: 74 us
  Pallas kernels  73.4 us (99%)
    pallas_call x1, Pallas kernels, on_device(): pl.pallas_call(attention_kernel, out_shape=(full,) * 4, in_specs=[pl.Bloc...  72.6 us

profile of v6, /device:TPU:1, one launch (start us, length us, event | category | flops | bytes accessed | tf_op | source)
XLA Modules:
  0.0 74.0 jit_solution(17183677610638025756)
XLA Ops:
  0.6 72.6 %attention.1 = (bf16[128,512]{1,0:T(8,128)(2,1)S(1)}, bf16[128,512]{1,0:T(8,128)(2,1)S(1)}, bf16[128,512]{1,0:T(8,128)(2,1)S(1)}, bf16[128,512]{1,0:T(8,128)(2,1)S(1)}) custom-call(s32[3,4,64]{2,1,0:T(4,128)} %bitcast.1, bf16[32,2048]{1,0:T(8,128)(2,1)} %q_ref.1, bf16[32,2048]{1,0:T(8,128)(2,1)} %k_ref.1, bf16[32,2048]{1,0:T(8,128)(2,1)} %v_ref.1, ...), custom_call_target="tpu_custom_call" | custom-call | tf_op jit(solution)/shard_map/attention/pallas_call | solution.py:545
  73.2 0.8 %place.1 = (bf16[128,512]{1,0:T(8,128)(2,1)}, bf16[128,512]{1,0:T(8,128)(2,1)}, bf16[128,512]{1,0:T(8,128)(2,1)}, bf16[128,512]{1,0:T(8,128)(2,1)}) custom-call(bf16[128,512]{1,0:T(8,128)(2,1)S(1)} %get-tuple-element.8.refs_0_, bf16[128,512]{1,0:T(8,128)(2,1)S(1)} %get-tuple-element.9.refs_1_, bf16[128,512]{1,0:T(8,128)(2,1)S(1)} %get-tuple-element.10.refs_2_, ...), custom_call_target="tpu_custom_call" | custom-call | tf_op jit(solution)/shard_map/place/pallas_call | solution.py:572

commit v7 on v6

--- a/solution.py
+++ b/solution.py
@@ -21,7 +21,7 @@
 ENTRIES = LEFT + 3
 SCALE = 1.0 / math.sqrt(HD)
 NEG = -1e30
-VMEM_LIMIT = 32 << 20
+VMEM_LIMIT = 44 << 20
 MESH = pl.DeviceIdType.MESH
 NT = (((1,), (1,)), ((), ()))
 NN = (((1,), (0,)), ((), ()))
@@ -54,7 +54,7 @@
 
 def attention_kernel(rb_in, q_ref, k_ref, v_ref, g_ref, o_out, dq_out, dk_out, dv_out,
                      kall0, kall1, vall0, vall1, qrow0, qrow1, grow0, grow1, sets, stats, rows, acc, wide_acc, own_acc, o_acc, dq_acc,
-                     zin, zsum, xin, xsum, zfin, xfin, final, gift, rb_ref, owner_s, prev_s, last_s, rb_sem,
+                     zin, zsum, xin, xsum, zfin, xfin, final, gift, kept_e, kept_p, rb_ref, owner_s, prev_s, last_s, rb_sem,
                      a_send, a_recv, a_own, g_send, g_recv, g_own, z_send, z_recv, x_send, x_recv, s_send, s_recv,
                      rz_send, rz_recv, rx_send, rx_recv, lz_send, lz_recv, lx_send, lx_recv, f_send, f_recv):
     s = lax.axis_index("seq")
@@ -234,15 +234,19 @@
         scores = pieces(dot(stack([k for k, _ in ks]), q, NT), len(ks))
         return [sc * SCALE if bias is None else sc * SCALE + bias for sc, (_, bias) in zip(scores, ks)]
 
-    def measure(ks, vs, q, g):
+    def measure(ks, vs, q, g, keep=None):
         scores = score(ks, q)
         peak = scores[0]
         for sc in scores[1:]:
             peak = jnp.maximum(peak, sc)
         peak = jnp.max(peak, axis=0, keepdims=True)
         total = weighted = None
-        for sc, dp in zip(scores, pieces(dot(stack(vs), g, NT), len(vs))):
+        for n, (sc, dp) in enumerate(zip(scores, pieces(dot(stack(vs), g, NT), len(vs)))):
             e = jnp.exp(sc - peak)
+            if keep is not None:
+                h, i = keep
+                kept_e[h, i, n] = e
+                kept_p[h, i, n] = dp
             w = e * dp
             total = e if total is None else total + e
             weighted = w if weighted is None else weighted + w
@@ -267,7 +271,7 @@
     def count_units(h, units):
         for i in units:
             ks, vs = tiles_of(h, i)
-            for n, row in enumerate(measure(ks, vs, qrow[h][i], grow[h][i])):
+            for n, row in enumerate(measure(ks, vs, qrow[h][i], grow[h][i], (h, i))):
                 sets[h, 0, n, i:i + 1, :] = row
 
     def count_rest(h):
@@ -312,9 +316,22 @@
             w = jnp.exp(sc - peak) * inverse
             wb.append(w.astype(BF16))
             ds.append((w * (dp - delta)).astype(BF16))
+        return spread(wb, ds, ks, vs, q, g)
+
+    def spread(wb, ds, ks, vs, q, g):
         wb, ds = stack(wb), stack(ds)
         k, v = stack([k for k, _ in ks]), stack(vs)
         return dot(ds, q, NN), dot(wb, g, NN), dot(wb, v, TN), dot(ds, k, TN)
+
+    def reweigh(h, i, ks, vs, q, g):
+        peak, inverse, delta = row_of(h, i)
+        factor = jnp.exp(sets[h, 0, 0, i:i + 1, :] - peak) * inverse
+        wb, ds = [], []
+        for n in range(len(ks)):
+            w = kept_e[h, i, n] * factor
+            wb.append(w.astype(BF16))
+            ds.append((w * (kept_p[h, i, n] - delta)).astype(BF16))
+        return spread(wb, ds, ks, vs, q, g)
 
     def row_of(h, i):
         return [rows[h, n, pl.ds(i, 1), :] for n in range(3)]
@@ -328,7 +345,7 @@
     def grad_units(h, units):
         for i in units:
             ks, vs = tiles_of(h, i)
-            dks, dvs, o, dq = weigh(ks, vs, qrow[h][i], grow[h][i], row_of(h, i))
+            dks, dvs, o, dq = reweigh(h, i, ks, vs, qrow[h][i], grow[h][i])
             for r, (dk, dv) in enumerate(zip(pieces(dks, len(ks)), pieces(dvs, len(vs)))):
                 if r < RAND:
                     store_entry(h, RAND * i + r, dk, dv)
@@ -556,6 +573,7 @@
             mem((2, 2, xs, 2, 2) + tile, BF16), mem((2, 2, xs, 2, 2) + tile, BF16),
             mem((2, 2, 2, 2) + tile, BF16), mem((2, 2, 2, 2) + tile, BF16),
             mem((2, 4) + tile, BF16), mem((2, 4) + tile, BF16),
+            mem((2, ROW, RAND + 1) + tile, F32), mem((2, ROW, RAND + 1) + tile, F32),
             pltpu.SMEM((RAND, 4, NX * COL), jnp.int32),
             pltpu.SMEM((2 * ENTRIES,), jnp.int32), pltpu.SMEM((2 * ENTRIES,), jnp.int32), pltpu.SMEM((2 * COL,), jnp.int32), dma,
             dma((2, 3, 2 * NY)), dma((2, 3, 2 * NY)), dma((2, 3)), dma((2,)), dma((2,)), dma((2,)),

time: 74.2 us -> 73.6 us (level)
  no operation moved by 1% of the time
where the time goes in v7:
time: 73.6 us; the launch traced here: 73.5 us
  Pallas kernels  72.9 us (99%)
    pallas_call x1, Pallas kernels, on_device(): pl.pallas_call(attention_kernel, out_shape=(full,) * 4, in_specs=[pl.Bloc...  72.1 us

profile of v7, /device:TPU:1, one launch (start us, length us, event | category | flops | bytes accessed | tf_op | source)
XLA Modules:
  0.0 73.5 jit_solution(8243896549389924379)
XLA Ops:
  0.6 72.1 %attention.1 = (bf16[128,512]{1,0:T(8,128)(2,1)S(1)}, bf16[128,512]{1,0:T(8,128)(2,1)S(1)}, bf16[128,512]{1,0:T(8,128)(2,1)S(1)}, bf16[128,512]{1,0:T(8,128)(2,1)S(1)}) custom-call(s32[3,4,64]{2,1,0:T(4,128)} %bitcast.1, bf16[32,2048]{1,0:T(8,128)(2,1)} %q_ref.1, bf16[32,2048]{1,0:T(8,128)(2,1)} %k_ref.1, bf16[32,2048]{1,0:T(8,128)(2,1)} %v_ref.1, ...), custom_call_target="tpu_custom_call" | custom-call | tf_op jit(solution)/shard_map/attention/pallas_call | solution.py:562
  72.7 0.8 %place.1 = (bf16[128,512]{1,0:T(8,128)(2,1)}, bf16[128,512]{1,0:T(8,128)(2,1)}, bf16[128,512]{1,0:T(8,128)(2,1)}, bf16[128,512]{1,0:T(8,128)(2,1)}) custom-call(bf16[128,512]{1,0:T(8,128)(2,1)S(1)} %get-tuple-element.8.refs_0_, bf16[128,512]{1,0:T(8,128)(2,1)S(1)} %get-tuple-element.9.refs_1_, bf16[128,512]{1,0:T(8,128)(2,1)S(1)} %get-tuple-element.10.refs_2_, ...), custom_call_target="tpu_custom_call" | custom-call | tf_op jit(solution)/shard_map/place/pallas_call | solution.py:590

commit v8 on v7

--- a/solution.py
+++ b/solution.py
@@ -423,10 +423,10 @@
                 go(h, direction, 1, 1 - direction)
 
         def step_on(h, step):
-            for t in (1, 0):
+            for ahead in (1, 0):
                 for direction in range(2):
-                    if not (step == 1 and t != direction):
-                        go(h, direction, step, t)
+                    if not (step == 1 and ahead):
+                        go(h, direction, step, direction ^ ahead)
 
         def ended(h, t, core):
             total = None

time: 73.6 us -> 72.9 us (level)
  no operation moved by 1% of the time
where the time goes in v8:
time: 72.9 us; the launch traced here: 72.8 us
  Pallas kernels  72.2 us (99%)
    pallas_call x1, Pallas kernels, on_device(): pl.pallas_call(attention_kernel, out_shape=(full,) * 4, in_specs=[pl.Bloc...  71.4 us

profile of v8, /device:TPU:1, one launch (start us, length us, event | category | flops | bytes accessed | tf_op | source)
XLA Modules:
  0.0 72.8 jit_solution(2224767148156935329)
XLA Ops:
  0.6 71.4 %attention.1 = (bf16[128,512]{1,0:T(8,128)(2,1)S(1)}, bf16[128,512]{1,0:T(8,128)(2,1)S(1)}, bf16[128,512]{1,0:T(8,128)(2,1)S(1)}, bf16[128,512]{1,0:T(8,128)(2,1)S(1)}) custom-call(s32[3,4,64]{2,1,0:T(4,128)} %bitcast.1, bf16[32,2048]{1,0:T(8,128)(2,1)} %q_ref.1, bf16[32,2048]{1,0:T(8,128)(2,1)} %k_ref.1, bf16[32,2048]{1,0:T(8,128)(2,1)} %v_ref.1, ...), custom_call_target="tpu_custom_call" | custom-call | tf_op jit(solution)/shard_map/attention/pallas_call | solution.py:562
  72.0 0.8 %place.1 = (bf16[128,512]{1,0:T(8,128)(2,1)}, bf16[128,512]{1,0:T(8,128)(2,1)}, bf16[128,512]{1,0:T(8,128)(2,1)}, bf16[128,512]{1,0:T(8,128)(2,1)}) custom-call(bf16[128,512]{1,0:T(8,128)(2,1)S(1)} %get-tuple-element.8.refs_0_, bf16[128,512]{1,0:T(8,128)(2,1)S(1)} %get-tuple-element.9.refs_1_, bf16[128,512]{1,0:T(8,128)(2,1)S(1)} %get-tuple-element.10.refs_2_, ...), custom_call_target="tpu_custom_call" | custom-call | tf_op jit(solution)/shard_map/place/pallas_call | solution.py:590

commit v9 on v8

--- a/solution.py
+++ b/solution.py
@@ -466,6 +466,9 @@
     exchange(0, 0)
     exchange(0, 1)
     exchange(1, 0)
+    lists.wait()
+    plan(0)
+    plan(1)
     zstart(0, 0)
     exchange(1, 1)
     zstart(0, 1)
@@ -477,15 +480,12 @@
     zstep(0, 0)
     zstart(1, 1)
     xstart(0)
-    lists.wait()
-    plan(0)
     zstep(0, 1)
     zstep(1, 0, (0,))
     xstart(1)
     xstep(0)
     zstep(0, 2)
     zstep(1, 0, (1,))
-    plan(1)
     xend(0)
     zend(0)
     pairs = [(i, i + 1) for i in range(0, ROW, 2)]
@@ -525,15 +525,15 @@
     grad_rim(1)
     zbegin(1)
     xbegin(1)
+    grad_own(1)
     zsum_on(0, 3)
-    grad_own(1)
-    give(1, range(4))
     zsum_on(1, 1)
     xsum_on(1, 1)
+    give(1, range(4))
+    zsum_on(1, 2)
     finish(0, (0, 1))
-    zsum_on(1, 2)
+    finish(1, (0, 1))
     finish(0, (2, 3))
-    finish(1, (0, 1))
     zsum_on(1, 3)
     finish(1, (3, 2))
     for cp in sends:

time: 72.9 us -> 72.9 us (level)
  no operation moved by 1% of the time
where the time goes in v9:
time: 72.9 us; the launch traced here: 72.7 us
  Pallas kernels  72.1 us (99%)
    pallas_call x1, Pallas kernels, on_device(): pl.pallas_call(attention_kernel, out_shape=(full,) * 4, in_specs=[pl.Bloc...  71.3 us

profile of v9, /device:TPU:1, one launch (start us, length us, event | category | flops | bytes accessed | tf_op | source)
XLA Modules:
  0.0 72.7 jit_solution(16139811716494146257)
XLA Ops:
  0.6 71.3 %attention.1 = (bf16[128,512]{1,0:T(8,128)(2,1)S(1)}, bf16[128,512]{1,0:T(8,128)(2,1)S(1)}, bf16[128,512]{1,0:T(8,128)(2,1)S(1)}, bf16[128,512]{1,0:T(8,128)(2,1)S(1)}) custom-call(s32[3,4,64]{2,1,0:T(4,128)} %bitcast.1, bf16[32,2048]{1,0:T(8,128)(2,1)} %q_ref.1, bf16[32,2048]{1,0:T(8,128)(2,1)} %k_ref.1, bf16[32,2048]{1,0:T(8,128)(2,1)} %v_ref.1, ...), custom_call_target="tpu_custom_call" | custom-call | tf_op jit(solution)/shard_map/attention/pallas_call | solution.py:562
  71.9 0.8 %place.1 = (bf16[128,512]{1,0:T(8,128)(2,1)}, bf16[128,512]{1,0:T(8,128)(2,1)}, bf16[128,512]{1,0:T(8,128)(2,1)}, bf16[128,512]{1,0:T(8,128)(2,1)}) custom-call(bf16[128,512]{1,0:T(8,128)(2,1)S(1)} %get-tuple-element.8.refs_0_, bf16[128,512]{1,0:T(8,128)(2,1)S(1)} %get-tuple-element.9.refs_1_, bf16[128,512]{1,0:T(8,128)(2,1)S(1)} %get-tuple-element.10.refs_2_, ...), custom_call_target="tpu_custom_call" | custom-call | tf_op jit(solution)/shard_map/place/pallas_call | solution.py:590
